TPU v7x, 32 devices: a whole 2x2x4 slice. The times are simulated.
32 devices in a mesh: dp: 16 (over z, y, x), expert: 2 (over core).
Axes of the slice: x: 2, y: 2, z: 4, core: 2. Of those that a mesh axis runs over, the one named last changes fastest.
Arguments:
- hidden: bfloat16 [2, 16384, 1024], P('expert', 'dp'), may hold values from -6 to 6
- cotangent: bfloat16 [2, 16384, 3584], P('expert', 'dp'), may hold values from -6 to 6
- counts: int32 [2, 16], P('expert', 'dp'), may hold values from 1 to 1024, as said below
- placement: int32 [2, 4], replicated, may hold values from 0 to 1, as said below
- weight: bfloat16 [2, 1024, 3584], P('expert', 'dp'), may hold values from -4 to 4
- moment: float32 [2, 1024, 3584], P('expert', 'dp'), may hold values from -2 to 2
- second: float32 [2, 1024, 3584], P('expert', 'dp'), may hold values from 0.005 to 1
- serving: bfloat16 [2, 4, 1024, 3584], P('expert', None, 'dp'), may hold values from -4 to 4
Outputs:
- d_hidden: bfloat16 [2, 16384, 1024], P('expert', 'dp')
- new_weight: bfloat16 [2, 1024, 3584], P('expert', 'dp')
- new_moment: float32 [2, 1024, 3584], P('expert', 'dp')
- new_second: float32 [2, 1024, 3584], P('expert', 'dp')
- served: bfloat16 [2, 4, 1024, 3584], P('expert', None, 'dp')
Inputs may be any that keep to these rules, and one draw needn't show every extreme that they name: `counts`: every count is reached by some expert and data shard in every draw at its upper end, 1024. `placement`: some two groups hold different experts as their first replica.
All inputs are finite; a program needn't handle non-finite values.
Results may differ from a plain program's by a relative error of at most 0.0012.
Values may be sent and summed in bfloat16 or wider, within the bound.
No kernel may reach another device: no remote copies, remote signals or barrier semaphores. Data moves between devices by JAX's collectives and lax.ppermute only.
A program may use at most 128 MiB of HBM per device.

v0:
```python
import jax
import jax.numpy as jnp
from jax import lax
from jax.sharding import PartitionSpec as P

D = 3584


beta_one = 0.9
beta_two = 0.95
bias_one = 1.0 - 0.9**20
bias_two = 1.0 - 0.95**20
learn_rate = 0.05
decay_rate = 0.1
epsilon = 1e-08


def on_device(hidden, cotangent, counts, placement, weight, moment, second, serving):
    scale = D ** (-0.5)
    acts = hidden[0]
    grads_out = cotangent[0]
    matrix = weight[0]
    tokens = acts.shape[0]
    owned = matrix.shape[0]
    width = matrix.shape[1]
    live = jnp.arange(tokens, dtype=jnp.int32) < counts[0, 0]
    masked = jnp.where(live[:, None], grads_out, jnp.zeros_like(grads_out))
    d_full = scale * jnp.dot(
        masked,
        lax.all_gather(matrix, "dp", axis=0, tiled=True).T,
        preferred_element_type=jnp.float32,
    )
    d_hid = d_full.astype(jnp.bfloat16)
    full_term = scale * jnp.dot(acts.T, masked, preferred_element_type=jnp.float32)
    grad = lax.psum_scatter(full_term, "dp", scatter_dimension=0, tiled=True)
    first_new = beta_one * moment[0] + (1.0 - beta_one) * grad
    squares_new = beta_two * second[0] + (1.0 - beta_two) * grad * grad
    step = first_new / bias_one / (jnp.sqrt(squares_new / bias_two) + epsilon)
    current = matrix.astype(jnp.float32)
    updated = current - learn_rate * (step + decay_rate * current)
    delta = (updated - current).astype(jnp.bfloat16)
    groups = lax.axis_size("expert")
    flat = delta.reshape(groups, -1)
    spread = lax.all_to_all(flat, "expert", split_axis=0, concat_axis=0, tiled=True)
    chosen = jnp.take(spread, placement.T, axis=0)
    arrived = lax.all_to_all(chosen, "expert", split_axis=1, concat_axis=1, tiled=True)
    copies = arrived.shape[0]
    incoming = arrived.reshape(copies, owned, width)
    served = (serving[0].astype(jnp.float32) + incoming.astype(jnp.float32)).astype(jnp.bfloat16)
    return (
        d_hid[None],
        updated.astype(jnp.bfloat16)[None],
        first_new[None],
        squares_new[None],
        served[None],
    )


def solution(mesh):
    placed = (
        P("expert", "dp", None),
        P("expert", "dp", None),
        P("expert", "dp"),
        P(),
        P("expert", "dp", None),
        P("expert", "dp", None),
        P("expert", "dp", None),
        P("expert", None, "dp", None),
    )
    return jax.shard_map(
        on_device,
        mesh=mesh,
        in_specs=placed,
        out_specs=(
            P("expert", "dp", None),
            P("expert", "dp", None),
            P("expert", "dp", None),
            P("expert", "dp", None),
            P("expert", None, "dp", None),
        ),
        check_vma=False,
    )
```

profile of v0, /device:TPU:11, one launch (start us, length us, event | category | flops | bytes accessed | tf_op | source)
XLA Modules:
  0.0 485.6 jit_solution(1999597831235390767)
XLA Ops:
  7.2 0.7 all-gather.3.cloned.1.call-update
  8.6 0.1 copy-done
  8.8 14.4 %multiply_bitcast_fusion = f32[1024,3584]{0,1:T(8,128)} fusion(bf16[1,1024,3584]{2,1,0:T(8,128)(2,1)} %param.9, pred[1024]{0:T(1024)(128)(4,1)S(1)} %iota_compare_fusion, bf16[1,1024,1024]{2,1,0:T(8,128)(2,1)S(1)} %copy-done), kind=kOutput, calls=%fused_computation.1 | convolution fusion | flops 7523532800 | bytes 24118272 | tf_op jit(solution)/shard_map/dot_general | solution.py:34
  23.1 14.4 %copy.51 = f32[1024,3584]{1,0:T(8,128)} copy(f32[1024,3584]{0,1:T(8,128)} %multiply_bitcast_fusion) | data formatting | bytes 29360128
  37.6 1.0 copy-done.3
  38.6 1.2 copy.40
  39.8 0.5 copy.41
  40.3 3.3 copy.42
  43.6 0.1 copy.45
  43.8 68.4 %all-gather.3.cloned.1.call-done = bf16[1,1024,3584]{2,1,0:T(8,128)(2,1)} async-done(((bf16[1,64,3584]{2,1,0:T(8,128)(2,1)}), bf16[1,1024,3584]{2,1,0:T(8,128)(2,1)}) %all-gather.3.cloned.1.call-update) | async-done | bytes 7340048 | tf_op jit(solution)/shard_map/all_gather | solution.py:30
  112.2 13.2 %fusion.15 = bf16[1,1024,1024]{2,1,0:T(8,128)(2,1)} fusion(bf16[1,1024,3584]{2,1,0:T(8,128)(2,1)} %all-gather.3.cloned.1.call-done, bf16[1,1024,3584]{2,1,0:T(8,128)(2,1)} %param.9, pred[1024]{0:T(1024)(128)(4,1)S(1)} %iota_compare_fusion), kind=kOutput, calls=%fused_computation.24 | convolution fusion | flops 7521959936 | bytes 16778240 | tf_op jit(solution)/shard_map/dot_general | solution.py:28
  125.4 299.0 %reduce-scatter.4.cloned.1.call-done = f32[64,3584]{1,0:T(8,128)} async-done(((f32[1024,3584]{1,0:T(8,128)}), f32[64,3584]{1,0:T(8,128)}) %reduce-scatter.4.cloned.1.call-update) | async-done | bytes 917520
  424.4 2.9 copy.52
  427.4 5.5 %fusion.14 = (bf16[64,3584]{0,1:T(8,128)(2,1)}, bf16[64,3584]{0,1:T(8,128)(2,1)S(1)}, f32[1,64,3584]{1,2,0:T(8,128)}, f32[1,64,3584]{1,2,0:T(8,128)}) fusion(bf16[1,64,3584]{1,2,0:T(8,128)(2,1)} %copy.40, f32[64,3584]{0,1:T(8,128)} %copy.52, f32[1,64,3584]{1,2,0:T(8,128)} %copy.42, f32[1,64,3584]{1,2,0:T(8,128)S(1)} %copy.41), kind=kLoop, calls=%fused_computation.21 | loop fusion | flops 4358144 | bytes 5963776 | tf_op jit(solution)/shard_map/convert_element_type | solution.py:41
  432.9 1.5 copy.43
  434.4 0.4 all_to_all.15
  434.8 0.5 broadcast.53
  435.3 3.9 reduce
  439.2 0.3 reshape.63
  439.6 4.8 all_to_all.18
  444.4 0.4 reshape.64
  444.8 0.7 copy.56
  445.5 3.0 gather_fusion
  448.5 2.6 reshape.50
  451.2 2.5 copy_select_fusion
  453.6 5.3 %all_to_all.19 = bf16[4,2,114688]{2,0,1:T(4,128)(2,1)S(1)} all-to-all(bf16[4,2,114688]{2,0,1:T(4,128)(2,1)S(1)} %copy_select_fusion), channel_id=1, replica_groups=mesh['dp'=16,'expert'=2] {'expert'}, dimensions={1} | all-to-all | bytes 3670016 | tf_op jit(solution)/shard_map/all_to_all | solution.py:46
  459.0 3.7 copy.47
  462.7 6.1 %reshape.48 = f32[1,4,64,3584]{3,2,1,0:T(8,128)} reshape(f32[4,2,114688]{2,1,0:T(2,128)} %copy.47) | data formatting | bytes 7340032 | tf_op jit(solution)/shard_map/convert_element_type | solution.py:49
  468.7 3.1 copy.49
  471.8 1.4 copy.50
  473.3 1.1 copy.48
  474.3 4.4 add_convert_fusion
  (18 shorter events, 0.2 us)
Async XLA Ops:
  7.2 1.6 copy-start
  7.2 105.0 %all-gather.3.cloned.1.call-start = ((), (), s32[]{:S(2)}) async-start(), calls=%async_computation.3 | async-start | bytes 7798784 | tf_op jit(solution)/shard_map/all_gather | solution.py:30
  7.9 416.5 %reduce-scatter.4.cloned.1.call-start = ((), (), s32[]{:S(2)}) async-start(), calls=%async_computation.4 | async-start | bytes 15597568
  37.5 1.0 copy-start.3
  38.6 1.2 copy-start.4
  40.3 3.3 copy-start.5
  468.7 3.1 copy-start.2
  474.3 4.4 copy-start.1
Sparse Core Ops, SparseCore 0:
  10.7 101.4 all-gather.2
  114.5 309.8 reduce-scatter.3
where the time goes:
time: 486 us
  waiting for transfers between devices  368 us (76%)
  local copies, waits for them, and re-layouts  48.6 us (10%)
  matrix products  27.6 us (6%)
  other arithmetic  16.3 us (3%)
  between operations  14.8 us (3%)
  blocking collectives  10.1 us (2%)
    unnamed x3, waiting for transfers between devices  300 us
    all_gather x1, waiting for transfers between devices, on_device(): lax.all_gather(matrix, 'dp', axis=0, tiled=True)  68.4 us
    unnamed x23, local copies, waits for them, and re-layouts  30.6 us
    dot_general x1, matrix products, on_device(): jnp.dot(acts.T, masked, preferred_element_type=jnp.float32)  14.4 us
    dot_general x1, matrix products, on_device(): jnp.dot(masked, lax.all_gather(matrix, 'dp', axis=0, tiled=True).T, prefe...  13.2 us
    convert_element_type x2, local copies, waits for them, and re-layouts, on_device(): incoming.astype(jnp.float32)  9.78 us
  transfers between devices with their start and end apart: 2, of which 2 were waited for; matrix products, arithmetic and copies ran while one was open for 10% of the time, Pallas kernels for 0%

commit v1 on v0

v1 whole, which is shorter than its diff:
```python
import functools
import math

import jax
import jax.numpy as jnp
from jax import lax
from jax.experimental import pallas as pl
from jax.experimental.pallas import tpu as pltpu
from jax.sharding import PartitionSpec as P


beta_one = 0.9
beta_two = 0.95
bias_one = 1.0 - 0.9**20
bias_two = 1.0 - 0.95**20
learn_rate = 0.05
decay_rate = 0.1
epsilon = 1e-08
largest_input = 6.0
half_range = 60000.0


def pairs_across(count, bit):
    return [(i, i ^ bit) for i in range(count)]


def pairs_around(count, k):
    return [((i + 4 * k) % count, i) for i in range(count)]


def pairs_along(count, step, first, last):
    return [(i, i + step * 4) for i in range(count) if first <= i // 4 < last]


def move(value, pairs, axis="dp"):
    return lax.ppermute(value, axis, pairs)


def after(value, *earlier):
    return lax.optimization_barrier((value,) + earlier)[0] if earlier else value


def pick(stacked, at, axis=0):
    return lax.dynamic_index_in_dim(stacked, at, axis, keepdims=False)


def gather_groups(depth):
    groups = {}
    for k in range(depth):
        groups.setdefault(max(k, depth - k) if k else 0, []).append(k)
    return [groups[t] for t in sorted(groups)]


def reduce_groups(depth):
    offsets = list(range(1, depth)) + [0]
    return [offsets[: depth // 2], offsets[depth // 2 :]]


def rows_kernel(order, place, limit, acts, send, keep, turned):
    depth = 2 * len(order[0])
    half = turned.shape[0] // (8 * depth)
    outer, upper, lower = place[0] // 4, lax.rem(place[0] // 2, 2), lax.rem(place[0], 2)
    values = acts[...]
    at = lax.broadcasted_iota(jnp.int32, values.shape, 0)
    turned[...] = jnp.where(at < limit[0], values, jnp.zeros_like(values)).T
    for out, flipped in ((send, 1), (keep, 0)):
        target = 0
        for g, h in ((0, 0), (0, 1), (1, 0), (1, 1)):
            for k in order[g]:
                z = lax.rem(outer + k, depth)
                for j in range(2):
                    y = upper ^ (1 - j) if h == 0 else upper ^ flipped
                    x = lower ^ flipped if h == 0 else lower ^ (1 - j)
                    source = (((z * 2 + y) * 2 + x) * 2 + h) * half
                    out[pl.ds(target, half)] = turned[pl.ds(pl.multiple_of(source, half), half)]
                    target += half


def rows_by_owner(order, place, limit, acts):
    tokens, rows = acts.shape
    shape = jax.ShapeDtypeStruct((rows // 2, tokens), acts.dtype)
    return pl.pallas_call(
        functools.partial(rows_kernel, order),
        out_shape=(shape, shape),
        grid_spec=pltpu.PrefetchScalarGridSpec(
            num_scalar_prefetch=2,
            grid=(1,),
            in_specs=[pl.BlockSpec((tokens, rows), lambda i, *_: (0, 0))],
            out_specs=[pl.BlockSpec((rows // 2, tokens), lambda i, *_: (0, 0))] * 2,
            scratch_shapes=[pltpu.VMEM((rows, tokens), acts.dtype)],
        ),
        name="rows_by_owner",
    )(place, limit, acts)


def hidden_kernel(groups, place, limit, *refs):
    columns, out, full = refs[-3:]
    upper, lower = lax.rem(place[0] // 2, 2), lax.rem(place[0], 2)
    half = full.shape[1] // 8

    def at(y, x, h):
        return pl.ds(pl.multiple_of(((y * 2 + x) * 2 + h) * half, half), half)

    start = 0
    for size in groups:
        far_a, far_b = refs[size : size + 2]
        for m in range(size):
            n = start + m
            near = refs[m]

            @pl.when((pl.program_id(0) == 0) & (pl.program_id(1) == n))
            def _():
                for j in range(2):
                    y, x = upper ^ j, lower ^ j
                    full[n, at(y, lower, 0)] = near[0, j]
                    full[n, at(y, 1 - lower, 0)] = far_a[m, j]
                    full[n, at(upper, x, 1)] = near[1, j]
                    full[n, at(1 - upper, x, 1)] = far_b[m, j]

        start += size
        refs = refs[size + 2 :]

    product = lax.dot_general(
        columns[...],
        full[pl.program_id(1)],
        (((1,), (1,)), ((), ())),
        preferred_element_type=jnp.float32,
    )
    product = columns.shape[1] ** (-0.5) * product
    first = pl.program_id(0) * product.shape[0]
    token = first + lax.broadcasted_iota(jnp.int32, product.shape, 0)
    out[...] = jnp.where(token < limit[0], product, 0.0).astype(out.dtype)


def hidden_columns(place, limit, groups, columns, so_far, depth):
    tokens, width = columns.shape
    offsets = [k for group, _ in groups for k in group]
    block = 8 * groups[0][1][0].shape[2]
    steps = 2

    def slot(place, k):
        return lax.rem(place[0] // 4 + k, depth)

    def same(array):
        zeros = (0,) * array.ndim
        return pl.BlockSpec(array.shape, lambda t, n, *_: zeros, pipeline_mode=pl.Buffered(1))

    in_specs, args = [], [place, limit]
    for _, arrays in groups:
        in_specs += [same(array) for array in arrays]
        args += arrays
    in_specs.append(pl.BlockSpec((tokens // steps, width), lambda t, n, *_: (t, 0)))
    args.append(columns)
    aliases = {}
    kernel = functools.partial(hidden_kernel, [len(group) for group, _ in groups])
    if so_far is not None:
        in_specs.insert(0, pl.BlockSpec(memory_space=pl.ANY))
        args.insert(2, so_far)
        aliases = {2: 0}
        inner = kernel
        kernel = lambda place, limit, so_far, *refs: inner(place, limit, *refs)

    def target(t, n, place, limit):
        at = slot(place, offsets[0])
        for m, k in enumerate(offsets[1:], 1):
            at = jnp.where(n == m, slot(place, k), at)
        return t, at

    return pl.pallas_call(
        kernel,
        out_shape=jax.ShapeDtypeStruct((tokens, depth * block), jnp.bfloat16),
        grid_spec=pltpu.PrefetchScalarGridSpec(
            num_scalar_prefetch=2,
            grid=(steps, len(offsets)),
            in_specs=in_specs,
            out_specs=pl.BlockSpec((tokens // steps, block), target),
            scratch_shapes=[pltpu.VMEM((len(offsets), block, width), jnp.bfloat16)],
        ),
        input_output_aliases=aliases,
        cost_estimate=pl.CostEstimate(
            flops=2 * tokens * width * block * len(offsets),
            transcendentals=0,
            bytes_accessed=2 * tokens * width,
        ),
        name="hidden_columns",
    )(*args)


def body(hidden, cotangent, counts, placement, weight, moment, second, serving):
    acts = hidden[0]
    grads_out = cotangent[0]
    matrix = weight[0]
    tokens, rows = acts.shape
    owned, width = matrix.shape
    scale = width ** (-0.5)
    count = lax.axis_size("dp")
    depth = count // 4
    index = lax.axis_index("dp")
    outer, upper, lower = index // 4, lax.rem(index // 2, 2), lax.rem(index, 2)
    half = owned // 2
    place = jnp.full((1,), index, jnp.int32)
    limit = counts[0]
    across_x, across_y = pairs_across(count, 1), pairs_across(count, 2)
    by_kernel = half % 16 == 0

    bound = count * tokens * largest_input**2 * scale
    lift = 2.0 ** math.floor(math.log2(half_range / bound))

    own_a, own_b = matrix[:half], matrix[half:]
    other_a = move(own_a, across_y)
    other_b = move(own_b, across_x)
    base = jnp.stack([jnp.stack([own_a, other_a]), jnp.stack([own_b, other_b])])
    below, above = {}, {}
    up = down = base
    for t in range(1, depth):
        up = below[t] = move(up, pairs_along(count, 1, t - 1, depth - 1))
        down = above[t] = move(down, pairs_along(count, -1, 1, depth - t + 1))
    near = {0: base}
    for k in range(1, depth):
        near[k] = jnp.where(outer + k < depth, above[k], below[depth - k])
    gathered = []
    for group in gather_groups(depth):
        far_a = move(jnp.stack([near[k][0] for k in group]), across_x)
        far_b = move(jnp.stack([near[k][1] for k in group]), across_y)
        gathered.append((group, [near[k] for k in group] + [far_a, far_b]))

    order = reduce_groups(depth)
    if by_kernel:
        send_rows, keep_rows = rows_by_owner(order, place, limit, acts)
    else:
        live = jnp.arange(tokens, dtype=jnp.int32) < limit[0]
        turned = jnp.where(live[:, None], acts, jnp.zeros_like(acts)).T
        turned = turned.reshape(depth, 2, 2, 2, half, tokens)
        turned = jnp.stack([pick(turned, lax.rem(outer + k, depth)) for k in sum(order, [])])

        def by_side(flipped):
            part_a = pick(turned[:, :, :, 0], lower ^ flipped, 2)
            part_b = pick(turned[:, :, :, 1], upper ^ flipped, 1)
            part_a = jnp.stack([pick(part_a, 1 - upper, 1), pick(part_a, upper, 1)], axis=1)
            part_b = jnp.stack([pick(part_b, 1 - lower, 1), pick(part_b, lower, 1)], axis=1)
            both = jnp.stack([part_a, part_b]).reshape(2, 2, depth // 2, 2, half, tokens)
            return jnp.swapaxes(both, 0, 1).reshape(-1, tokens)

        send_rows, keep_rows = by_side(1), by_side(0)

    def term(picked, kind):
        product = jnp.dot(picked, grads_out, preferred_element_type=jnp.float32)
        product = ((scale * lift) * product).astype(kind)
        return product.reshape(-1, 2, depth // 2, 2, half, width)

    def wide(value):
        return value.astype(jnp.float32)

    came = []
    for g in range(2):
        some = send_rows[g * rows // 4 : (g + 1) * rows // 4]
        send = term(some, jnp.float16)[0]
        came_a = move(send[0], across_x)
        came_b = move(send[1], across_y)
        came.append((came_a, came_b))
    keep = term(keep_rows, jnp.float32)
    sent, middle = (), []
    for g in range(2):
        came_a, came_b = came[g]
        kept = after(keep, *sent)
        out_a = (kept[g, 0, :, 0] + wide(came_a[:, 0])).astype(jnp.float16)
        out_b = (kept[g, 1, :, 0] + wide(came_b[:, 0])).astype(jnp.float16)
        second_a = move(out_a, across_y)
        second_b = move(out_b, across_x)
        middle.append((second_a, second_b))
        sent = (out_a, out_b)
    parts, total = [], None
    for g in range(2):
        came_a, came_b = came[g]
        second_a, second_b = (after(value, *sent) for value in middle[g])
        leaving = []
        for n, k in enumerate(order[g]):
            sum_a = keep[g, 0, n, 1] + wide(came_a[n, 1]) + wide(second_a[n])
            sum_b = keep[g, 1, n, 1] + wide(came_b[n, 1]) + wide(second_b[n])
            joined = jnp.concatenate([sum_a, sum_b])
            if k:
                leaving.append(joined.astype(jnp.float16))
            else:
                total = joined
            if k:
                parts.append(move(leaving[-1], pairs_around(count, depth - k)))
        sent = tuple(leaving)
    for value in parts:
        total = total + wide(value)
    grad = (1.0 / lift) * total

    first_new = beta_one * moment[0] + (1.0 - beta_one) * grad
    squares_new = beta_two * second[0] + (1.0 - beta_two) * grad * grad
    step = first_new / bias_one / (jnp.sqrt(squares_new / bias_two) + epsilon)
    current = matrix.astype(jnp.float32)
    updated = current - learn_rate * (step + decay_rate * current)
    delta = (updated - current).astype(jnp.bfloat16)

    groups = lax.axis_size("expert")
    mine = lax.axis_index("expert")
    wanted = pick(placement, mine)[:, None, None]
    incoming = jnp.where(wanted == mine, delta[None], jnp.zeros_like(delta)[None])
    for shift in range(1, groups):
        ring = [(e, (e + shift) % groups) for e in range(groups)]
        other = move(delta, ring, "expert")
        source = lax.rem(mine + groups - shift, groups)
        incoming = jnp.where(wanted == source, other[None], incoming)
    served = serving[0].astype(jnp.float32) + incoming.astype(jnp.float32)

    if by_kernel:
        d_hid = None
        for some in (gathered[:-1], gathered[-1:]):
            d_hid = hidden_columns(place, limit, some, grads_out, d_hid, depth)
    else:
        blocks = {}
        for group, arrays in gathered:
            far_a, far_b = arrays[len(group) :]
            for m, k in enumerate(group):
                full_a = jnp.stack([arrays[m][0], far_a[m]], axis=1)
                full_b = jnp.stack([arrays[m][1], far_b[m]], axis=0)
                blocks[k] = jnp.stack([full_a, full_b], axis=2)
        full = jnp.stack([blocks[k] for k in range(depth)] * 2)
        full = lax.dynamic_slice_in_dim(full, depth - outer, depth, 0)
        full = jnp.where(upper == 0, full, jnp.flip(full, 1))
        full = jnp.where(lower == 0, full, jnp.flip(full, 2)).reshape(rows, width)
        live = jnp.arange(tokens, dtype=jnp.int32) < limit[0]
        d_full = scale * jnp.dot(grads_out, full.T, preferred_element_type=jnp.float32)
        d_hid = jnp.where(live[:, None], d_full, 0.0).astype(jnp.bfloat16)
    return (
        d_hid[None],
        updated.astype(jnp.bfloat16)[None],
        first_new[None],
        squares_new[None],
        served.astype(jnp.bfloat16)[None],
    )


def solution(mesh):
    placed = (
        P("expert", "dp", None),
        P("expert", "dp", None),
        P("expert", "dp"),
        P(),
        P("expert", "dp", None),
        P("expert", "dp", None),
        P("expert", "dp", None),
        P("expert", None, "dp", None),
    )
    return jax.shard_map(
        body,
        mesh=mesh,
        in_specs=placed,
        out_specs=(
            P("expert", "dp", None),
            P("expert", "dp", None),
            P("expert", "dp", None),
            P("expert", "dp", None),
            P("expert", None, "dp", None),
        ),
        check_vma=False,
    )
```

time: 486 us -> 218 us (0.45)
  the two profiles are of different devices: /device:TPU:11 before, /device:TPU:16 now
where the time goes in v1:
time: 218 us
  waiting for transfers between devices  131 us (60%)
  starting transfers between devices  33.4 us (15%)
  Pallas kernels  23 us (11%)
  other arithmetic  13.6 us (6%)
  matrix products  11.5 us (5%)
  local copies, waits for them, and re-layouts  3.57 us (2%)
    ppermute x26, waiting for transfers between devices, move(): return lax.ppermute(value, axis, pairs)  131 us
    ppermute x26, starting transfers between devices, move(): return lax.ppermute(value, axis, pairs)  33.4 us
    pallas_call x2, Pallas kernels, hidden_columns(): pl.pallas_call(kernel, out_shape=jax.ShapeDtypeStruct((tokens, depth * bl...  19.2 us
    dot_general x3, matrix products, term(): product = jnp.dot(picked, grads_out, preferred_element_type=jnp.float32)  11.5 us
  transfers between devices with their start and end apart: 26, of which 11 were waited for; matrix products, arithmetic and copies ran while one was open for 9% of the time, Pallas kernels for 4%

profile of v1, /device:TPU:16, one launch (start us, length us, event | category | flops | bytes accessed | tf_op | source)
XLA Modules:
  0.0 217.9 jit_solution(3133844094716325366)
XLA Ops:
  1.3 3.8 %rows_by_owner.1 = (bf16[512,1024]{1,0:T(8,128)(2,1)}, bf16[512,1024]{1,0:T(8,128)(2,1)}) custom-call(s32[1]{0:T(128)} %bitcast.place, s32[1]{0:T(128)} %bitcast.222.limit, bf16[1024,1024]{1,0:T(8,128)(2,1)} %bitcast.232), custom_call_target="tpu_custom_call" | custom-call | tf_op jit(solution)/shard_map/rows_by_owner/pallas_call | solution.py:82
  5.1 5.5 %fusion.1 = f16[256,3584]{1,0:T(8,128)(2,1)S(1)} fusion(bf16[512,1024]{1,0:T(8,128)(2,1)} %get-tuple-element.13, bf16[1,1024,3584]{2,1,0:T(8,128)(2,1)} %param.9), kind=kOutput, calls=%fused_computation.4 | convolution fusion | flops 1880883200 | bytes 9699328 | tf_op jit(solution)/shard_map/dot_general | solution.py:247
  10.9 1.6 collective-permute-start.15
  12.4 1.5 collective-permute-start.16
  13.9 2.1 fusion
  17.7 1.6 collective-permute-start
  19.3 4.0 %convolution_multiply_fusion = f32[512,3584]{1,0:T(8,128)S(1)} fusion(bf16[512,1024]{1,0:T(8,128)(2,1)S(1)} %copy-done.12, bf16[1,1024,3584]{2,1,0:T(8,128)(2,1)S(1)} %bitcast.230), kind=kOutput, calls=%fused_computation | convolution fusion | flops 3759931392 | bytes 15728640 | tf_op jit(solution)/shard_map/dot_general | solution.py:247
  23.2 35.5 %collective-permute-done = bf16[32,3584]{1,0:T(8,128)(2,1)S(1)} collective-permute-done((bf16[32,3584]{1,0:T(8,128)(2,1)S(1)}, bf16[32,3584]{1,0:T(8,128)(2,1)S(1)}, u32[]{:S(2)}, u32[]{:S(2)}) %collective-permute-start) | collective-permute-done | bytes 229408 | tf_op jit(solution)/shard_map/ppermute | solution.py:36
  59.4 5.6 %collective-permute-done.1 = bf16[32,3584]{1,0:T(8,128)(2,1)S(1)} collective-permute-done((bf16[32,3584]{1,0:T(8,128)(2,1)S(1)}, bf16[32,3584]{1,0:T(8,128)(2,1)S(1)}, u32[]{:S(2)}, u32[]{:S(2)}) %collective-permute-start.1) | collective-permute-done | bytes 229408 | tf_op jit(solution)/shard_map/ppermute | solution.py:36
  66.9 3.5 %collective-permute-start.6 = (bf16[2,2,32,3584]{3,2,1,0:T(8,128)(2,1)}, bf16[2,2,32,3584]{3,2,1,0:T(8,128)(2,1)}, u32[]{:S(2)}, u32[]{:S(2)}) collective-permute-start(bf16[2,2,32,3584]{3,2,1,0:T(8,128)(2,1)} %pad_maximum_fusion.refs_0_), channel_id=1, source_target_pairs={{0,8},{2,10},{4,12},{6,14},{8,16},{10,18},{12,20},{14,22},{16,24},... | collective-permute-start | bytes 2752520 | tf_op jit(solution)/shard_map/ppermute | solution.py:36
  70.4 2.4 %collective-permute-start.4 = (bf16[2,2,32,3584]{3,2,1,0:T(8,128)(2,1)}, bf16[2,2,32,3584]{3,2,1,0:T(8,128)(2,1)}, u32[]{:S(2)}, u32[]{:S(2)}) collective-permute-start(bf16[2,2,32,3584]{3,2,1,0:T(8,128)(2,1)} %pad_maximum_fusion.refs_0_), channel_id=1, source_target_pairs={{8,0},{10,2},{12,4},{14,6},{16,8},{18,10},{20,12},{22,14},{24,16},... | collective-permute-start | bytes 2752520 | tf_op jit(solution)/shard_map/ppermute | solution.py:36
  73.6 1.5 collective-permute-start.18
  75.3 1.6 collective-permute-start.21
  76.8 9.6 %collective-permute-done.20 = f16[2,32,3584]{2,1,0:T(8,128)(2,1)S(1)} collective-permute-done((f16[2,32,3584]{2,1,0:T(8,128)(2,1)S(1)}, f16[2,32,3584]{2,1,0:T(8,128)(2,1)S(1)}, u32[]{:S(2)}, u32[]{:S(2)}) %collective-permute-start.20) | collective-permute-done | bytes 458784 | tf_op jit(solution)/shard_map/ppermute | solution.py:36
  90.1 2.5 %collective-permute-done.21 = f16[2,32,3584]{2,1,0:T(8,128)(2,1)S(1)} collective-permute-done((f16[2,32,3584]{2,1,0:T(8,128)(2,1)S(1)}, f16[2,32,3584]{2,1,0:T(8,128)(2,1)S(1)}, u32[]{:S(2)}, u32[]{:S(2)}) %collective-permute-start.21) | collective-permute-done | bytes 458784 | tf_op jit(solution)/shard_map/ppermute | solution.py:36
  92.6 2.3 %collective-permute-done.17 = f16[2,32,3584]{2,1,0:T(8,128)(2,1)S(1)} collective-permute-done((f16[2,32,3584]{2,1,0:T(8,128)(2,1)S(1)}, f16[2,32,3584]{2,1,0:T(8,128)(2,1)S(1)}, u32[]{:S(2)}, u32[]{:S(2)}) %collective-permute-start.17) | collective-permute-done | bytes 458784 | tf_op jit(solution)/shard_map/ppermute | solution.py:36
  97.5 3.5 %collective-permute-start.23 = (f16[64,3584]{1,0:T(8,128)(2,1)}, f16[64,3584]{1,0:T(8,128)(2,1)}, u32[]{:S(2)}, u32[]{:S(2)}) collective-permute-start(f16[64,3584]{1,0:T(8,128)(2,1)} %pad_maximum_fusion.4), channel_id=1, source_target_pairs={{16,0},{18,2},{20,4},{22,6},{24,8},{26,10},{28,12},{30,14},{0,16},... | collective-permute-start | bytes 1376264 | tf_op jit(solution)/shard_map/ppermute | solution.py:36
  101.6 1.5 collective-permute-start.3
  103.1 23.4 %collective-permute-done.24 = f16[64,3584]{1,0:T(8,128)(2,1)} collective-permute-done((f16[64,3584]{1,0:T(8,128)(2,1)}, f16[64,3584]{1,0:T(8,128)(2,1)}, u32[]{:S(2)}, u32[]{:S(2)}) %collective-permute-start.24) | collective-permute-done | bytes 458784 | tf_op jit(solution)/shard_map/ppermute | solution.py:36
  126.5 1.9 collective-permute-start.7
  128.4 6.7 %collective-permute-done.23 = f16[64,3584]{1,0:T(8,128)(2,1)} collective-permute-done((f16[64,3584]{1,0:T(8,128)(2,1)}, f16[64,3584]{1,0:T(8,128)(2,1)}, u32[]{:S(2)}, u32[]{:S(2)}) %collective-permute-start.23) | collective-permute-done | bytes 458784 | tf_op jit(solution)/shard_map/ppermute | solution.py:36
  136.5 2.3 %fusion.4 = (bf16[64,3584]{1,0:T(8,128)(2,1)S(1)}, bf16[64,3584]{1,0:T(8,128)(2,1)S(1)}, f32[64,3584]{1,0:T(8,128)S(1)}) fusion(bf16[1,64,3584]{2,1,0:T(8,128)(2,1)S(1)} %copy-done.6, f32[1,64,3584]{2,1,0:T(8,128)S(1)} %copy-done.3, f32[1,64,3584]{2,1,0:T(8,128)S(1)} %copy-done.4, f16[64,3584]{1,0:T(8,128)(2,1)} %collective-permute-done.24, ...), kind=kLoop, calls=%fused_computation.11 | loop fusion | flops 6193152 | bytes 6422528 | tf_op jit(solution)/shard_map/convert_element_type | solution.py:297
  138.9 1.6 fusion.38
  140.4 13.7 %collective-permute-done.7 = bf16[2,2,32,3584]{3,2,1,0:T(8,128)(2,1)S(1)} collective-permute-done((bf16[2,2,32,3584]{3,2,1,0:T(8,128)(2,1)}, bf16[2,2,32,3584]{3,2,1,0:T(8,128)(2,1)S(1)}, u32[]{:S(2)}, u32[]{:S(2)}) %collective-permute-start.7) | collective-permute-done | bytes 917536 | tf_op jit(solution)/shard_map/ppermute | solution.py:36
  154.1 1.5 collective-permute-start.10
  156.4 18.1 %collective-permute-done.10 = bf16[2,2,32,3584]{3,2,1,0:T(8,128)(2,1)S(1)} collective-permute-done((bf16[2,2,32,3584]{3,2,1,0:T(8,128)(2,1)S(1)}, bf16[2,2,32,3584]{3,2,1,0:T(8,128)(2,1)S(1)}, u32[]{:S(2)}, u32[]{:S(2)}) %collective-permute-start.10) | collective-permute-done | bytes 917536 | tf_op jit(solution)/shard_map/ppermute | solution.py:36
  176.6 1.6 collective-permute-start.9
  181.2 1.9 add_convert_fusion
  183.1 7.0 %collective-permute-done.9.refs_5_ = bf16[1,2,32,3584]{3,2,1,0:T(8,128)(2,1)S(1)} collective-permute-done((bf16[1,2,32,3584]{3,2,1,0:T(8,128)(2,1)S(1)}, bf16[1,2,32,3584]{3,2,1,0:T(8,128)(2,1)S(1)}, u32[]{:S(2)}, u32[]{:S(2)}) %collective-permute-start.9) | collective-permute-done | bytes 458784 | tf_op jit(solution)/shard_map/ppermute | solution.py:36
  190.9 9.6 %hidden_columns.2.so_far = bf16[1024,1024]{1,0:T(8,128)(2,1)} custom-call(s32[1]{0:T(128)} %bitcast.place, s32[1]{0:T(128)} %bitcast.220.limit, bf16[2,2,32,3584]{3,2,1,0:T(8,128)(2,1)} %pad_maximum_fusion.refs_0_, bf16[1,2,32,3584]{3,2,1,0:T(8,128)(2,1)} %copy-done.14, bf16[1,2,32,3584]{3,2,1,0:T(8,128)(2,1)} %copy-done.15, ...), custom_call_target="tpu_custom_call" | custom-call | flops 3758096384 | bytes 7340032 | tf_op jit(solution)/shard_map/hidden_columns/pallas_call | solution.py:169
  200.5 6.9 %collective-permute-done.13.refs_3_ = bf16[2,2,32,3584]{3,2,1,0:T(8,128)(2,1)S(1)} collective-permute-done((bf16[2,2,32,3584]{3,2,1,0:T(8,128)(2,1)S(1)}, bf16[2,2,32,3584]{3,2,1,0:T(8,128)(2,1)S(1)}, u32[]{:S(2)}, u32[]{:S(2)}) %collective-permute-start.13) | collective-permute-done | bytes 917536 | tf_op jit(solution)/shard_map/ppermute | solution.py:36
  208.3 9.6 %hidden_columns.3 = bf16[1024,1024]{1,0:T(8,128)(2,1)} custom-call(s32[1]{0:T(128)} %bitcast.place, s32[1]{0:T(128)} %bitcast.221.limit, bf16[1024,1024]{1,0:T(8,128)(2,1)} %hidden_columns.2.so_far, bf16[2,2,32,3584]{3,2,1,0:T(8,128)(2,1)} %copy-done, bf16[2,2,32,3584]{3,2,1,0:T(8,128)(2,1)} %copy-done.1, ...), custom_call_target="tpu_custom_call", output_to_operand_aliasing={{}: (2, {})} | custom-call | flops 3758096384 | bytes 7340032 | tf_op jit(solution)/shard_map/hidden_columns/pallas_call | solution.py:169
  (93 shorter events, 21.2 us)
Async XLA Ops:
  1.3 12.6 %slice-start = ((s8[7340032]{0:T(1024)(128)(4,1)}), s8[3145728]{0:T(1024)(128)(4,1)S(1)}, s32[]{:S(2)}) async-start(s8[7340032]{0:T(1024)(128)(4,1)} %bitcast.229), calls=%async_computation | async-start | bytes 6291456
  10.9 59.5 %collective-permute-start.15 = (f16[2,2,32,3584]{3,2,1,0:T(8,128)(2,1)S(1)}, f16[2,2,32,3584]{3,2,1,0:T(8,128)(2,1)S(1)}, u32[]{:S(2)}, u32[]{:S(2)}) collective-permute-start(f16[2,2,32,3584]{3,2,1,0:T(8,128)(2,1)S(1)} %bitcast.236), channel_id=1, source_target_pairs={{0,2},{2,0},{4,6},{6,4},{8,10},{10,8},{12,14},{14,12},{16,18},{18,... | collective-permute-start | bytes 2752520 | tf_op jit(solution)/shard_map/ppermute | solution.py:36
  12.4 60.3 %collective-permute-start.16 = (f16[2,2,32,3584]{3,2,1,0:T(8,128)(2,1)S(1)}, f16[2,2,32,3584]{3,2,1,0:T(8,128)(2,1)S(1)}, u32[]{:S(2)}, u32[]{:S(2)}) collective-permute-start(f16[2,2,32,3584]{3,2,1,0:T(8,128)(2,1)S(1)} %bitcast.235), channel_id=1, source_target_pairs={{0,4},{2,6},{4,0},{6,2},{8,12},{10,14},{12,8},{14,10},{16,20},{18,... | collective-permute-start | bytes 2752520 | tf_op jit(solution)/shard_map/ppermute | solution.py:36
  16.5 57.0 %collective-permute-start.19 = (f16[2,2,32,3584]{3,2,0,1:T(8,128)(2,1)S(1)}, f16[2,2,32,3584]{3,2,0,1:T(8,128)(2,1)S(1)}, u32[]{:S(2)}, u32[]{:S(2)}) collective-permute-start(f16[2,2,32,3584]{3,2,0,1:T(8,128)(2,1)S(1)} %copy.16), channel_id=1, source_target_pairs={{0,4},{2,6},{4,0},{6,2},{8,12},{10,14},{12,8},{14,10},{16,20},{18,... | collective-permute-start | bytes 2752520 | tf_op jit(solution)/shard_map/ppermute | solution.py:36
  17.1 58.0 %collective-permute-start.14 = (f16[2,2,32,3584]{3,2,1,0:T(8,128)(2,1)S(1)}, f16[2,2,32,3584]{3,2,1,0:T(8,128)(2,1)S(1)}, u32[]{:S(2)}, u32[]{:S(2)}) collective-permute-start(f16[2,2,32,3584]{3,2,1,0:T(8,128)(2,1)S(1)} %bitcast.234), channel_id=1, source_target_pairs={{0,2},{2,0},{4,6},{6,4},{8,10},{10,8},{12,14},{14,12},{16,18},{18,... | collective-permute-start | bytes 2752520 | tf_op jit(solution)/shard_map/ppermute | solution.py:36
  17.7 41.1 %collective-permute-start = (bf16[32,3584]{1,0:T(8,128)(2,1)S(1)}, bf16[32,3584]{1,0:T(8,128)(2,1)S(1)}, u32[]{:S(2)}, u32[]{:S(2)}) collective-permute-start(bf16[32,3584]{1,0:T(8,128)(2,1)S(1)} %get-tuple-element.52), channel_id=1, source_target_pairs={{0,4},{2,6},{4,0},{6,2},{8,12},{10,14},{12,8},{14,10},{16,20},{18,... | collective-permute-start | bytes 688136 | tf_op jit(solution)/shard_map/ppermute | solution.py:36
  58.8 6.2 %collective-permute-start.1 = (bf16[32,3584]{1,0:T(8,128)(2,1)S(1)}, bf16[32,3584]{1,0:T(8,128)(2,1)S(1)}, u32[]{:S(2)}, u32[]{:S(2)}) collective-permute-start(bf16[32,3584]{1,0:T(8,128)(2,1)S(1)} %get-tuple-element.51), channel_id=1, source_target_pairs={{0,2},{2,0},{4,6},{6,4},{8,10},{10,8},{12,14},{14,12},{16,18},{18,... | collective-permute-start | bytes 688136 | tf_op jit(solution)/shard_map/ppermute | solution.py:36
  66.9 34.2 %collective-permute-start.6 = (bf16[2,2,32,3584]{3,2,1,0:T(8,128)(2,1)}, bf16[2,2,32,3584]{3,2,1,0:T(8,128)(2,1)}, u32[]{:S(2)}, u32[]{:S(2)}) collective-permute-start(bf16[2,2,32,3584]{3,2,1,0:T(8,128)(2,1)} %pad_maximum_fusion.refs_0_), channel_id=1, source_target_pairs={{0,8},{2,10},{4,12},{6,14},{8,16},{10,18},{12,20},{14,22},{16,24},... | collective-permute-start | bytes 2752520 | tf_op jit(solution)/shard_map/ppermute | solution.py:36
  70.4 31.3 %collective-permute-start.4 = (bf16[2,2,32,3584]{3,2,1,0:T(8,128)(2,1)}, bf16[2,2,32,3584]{3,2,1,0:T(8,128)(2,1)}, u32[]{:S(2)}, u32[]{:S(2)}) collective-permute-start(bf16[2,2,32,3584]{3,2,1,0:T(8,128)(2,1)} %pad_maximum_fusion.refs_0_), channel_id=1, source_target_pairs={{8,0},{10,2},{12,4},{14,6},{16,8},{18,10},{20,12},{22,14},{24,16},... | collective-permute-start | bytes 2752520 | tf_op jit(solution)/shard_map/ppermute | solution.py:36
  73.0 13.5 %collective-permute-start.20 = (f16[2,32,3584]{2,1,0:T(8,128)(2,1)S(1)}, f16[2,32,3584]{2,1,0:T(8,128)(2,1)S(1)}, u32[]{:S(2)}, u32[]{:S(2)}) collective-permute-start(f16[2,32,3584]{2,1,0:T(8,128)(2,1)S(1)} %get-tuple-element.36), channel_id=1, source_target_pairs={{0,2},{2,0},{4,6},{6,4},{8,10},{10,8},{12,14},{14,12},{16,18},{18,... | collective-permute-start | bytes 1376264 | tf_op jit(solution)/shard_map/ppermute | solution.py:36
  73.6 14.4 %collective-permute-start.18 = (f16[2,32,3584]{2,1,0:T(8,128)(2,1)S(1)}, f16[2,32,3584]{2,1,0:T(8,128)(2,1)S(1)}, u32[]{:S(2)}, u32[]{:S(2)}) collective-permute-start(f16[2,32,3584]{2,1,0:T(8,128)(2,1)S(1)} %get-tuple-element.37), channel_id=1, source_target_pairs={{0,4},{2,6},{4,0},{6,2},{8,12},{10,14},{12,8},{14,10},{16,20},{18,... | collective-permute-start | bytes 1376264 | tf_op jit(solution)/shard_map/ppermute | solution.py:36
  75.3 17.3 %collective-permute-start.21 = (f16[2,32,3584]{2,1,0:T(8,128)(2,1)S(1)}, f16[2,32,3584]{2,1,0:T(8,128)(2,1)S(1)}, u32[]{:S(2)}, u32[]{:S(2)}) collective-permute-start(f16[2,32,3584]{2,1,0:T(8,128)(2,1)S(1)} %get-tuple-element.35), channel_id=1, source_target_pairs={{0,2},{2,0},{4,6},{6,4},{8,10},{10,8},{12,14},{14,12},{16,18},{18,... | collective-permute-start | bytes 1376264 | tf_op jit(solution)/shard_map/ppermute | solution.py:36
  86.4 8.5 %collective-permute-start.17 = (f16[2,32,3584]{2,1,0:T(8,128)(2,1)S(1)}, f16[2,32,3584]{2,1,0:T(8,128)(2,1)S(1)}, u32[]{:S(2)}, u32[]{:S(2)}) collective-permute-start(f16[2,32,3584]{2,1,0:T(8,128)(2,1)S(1)} %get-tuple-element.34), channel_id=1, source_target_pairs={{0,4},{2,6},{4,0},{6,2},{8,12},{10,14},{12,8},{14,10},{16,20},{18,... | collective-permute-start | bytes 1376264 | tf_op jit(solution)/shard_map/ppermute | solution.py:36
  89.2 11.8 %copy-start.11 = (s32[2,4]{1,0:T(2,128)S(1)}, s32[2,4]{1,0:T(2,128)}, u32[]{:S(2)}) copy-start(s32[2,4]{1,0:T(2,128)} %param.11) | copy-start | bytes 100
  89.2 47.3 %copy-start.3 = (f32[1,64,3584]{2,1,0:T(8,128)S(1)}, f32[1,64,3584]{2,1,0:T(8,128)}, u32[]{:S(2)}) copy-start(f32[1,64,3584]{2,1,0:T(8,128)} %param.14) | copy-start | bytes 2752516
  89.2 47.3 %copy-start.4 = (f32[1,64,3584]{2,1,0:T(8,128)S(1)}, f32[1,64,3584]{2,1,0:T(8,128)}, u32[]{:S(2)}) copy-start(f32[1,64,3584]{2,1,0:T(8,128)} %param.13) | copy-start | bytes 2752516
  89.2 47.3 %copy-start.6 = (bf16[1,64,3584]{2,1,0:T(8,128)(2,1)S(1)}, bf16[1,64,3584]{2,1,0:T(8,128)(2,1)}, u32[]{:S(2)}) copy-start(bf16[1,64,3584]{2,1,0:T(8,128)(2,1)} %param.12) | copy-start | bytes 1376260
  96.1 30.4 %collective-permute-start.24 = (f16[64,3584]{1,0:T(8,128)(2,1)}, f16[64,3584]{1,0:T(8,128)(2,1)}, u32[]{:S(2)}, u32[]{:S(2)}) collective-permute-start(f16[64,3584]{1,0:T(8,128)(2,1)} %pad_maximum_fusion.5), channel_id=1, source_target_pairs={{8,0},{10,2},{12,4},{14,6},{16,8},{18,10},{20,12},{22,14},{24,16},... | collective-permute-start | bytes 1376264 | tf_op jit(solution)/shard_map/ppermute | solution.py:36
  97.5 37.6 %collective-permute-start.23 = (f16[64,3584]{1,0:T(8,128)(2,1)}, f16[64,3584]{1,0:T(8,128)(2,1)}, u32[]{:S(2)}, u32[]{:S(2)}) collective-permute-start(f16[64,3584]{1,0:T(8,128)(2,1)} %pad_maximum_fusion.4), channel_id=1, source_target_pairs={{16,0},{18,2},{20,4},{22,6},{24,8},{26,10},{28,12},{30,14},{0,16},... | collective-permute-start | bytes 1376264 | tf_op jit(solution)/shard_map/ppermute | solution.py:36
  101.0 35.5 %collective-permute-start.22 = (f16[64,3584]{1,0:T(8,128)(2,1)}, f16[64,3584]{1,0:T(8,128)(2,1)}, u32[]{:S(2)}, u32[]{:S(2)}) collective-permute-start(f16[64,3584]{1,0:T(8,128)(2,1)} %pad_maximum_fusion.3), channel_id=1, source_target_pairs={{24,0},{26,2},{28,4},{30,6},{0,8},{2,10},{4,12},{6,14},{8,16},{10,... | collective-permute-start | bytes 1376264 | tf_op jit(solution)/shard_map/ppermute | solution.py:36
  101.0 78.8 %collective-permute-start.2 = (bf16[1,2,32,3584]{3,2,1,0:T(8,128)(2,1)}, bf16[1,2,32,3584]{3,2,1,0:T(8,128)(2,1)S(1)}, u32[]{:S(2)}, u32[]{:S(2)}) collective-permute-start(bf16[1,2,32,3584]{3,2,1,0:T(8,128)(2,1)} %copy-done.8), channel_id=1, source_target_pairs={{0,2},{2,0},{4,6},{6,4},{8,10},{10,8},{12,14},{14,12},{16,18},{18,... | collective-permute-start | bytes 1376264 | tf_op jit(solution)/shard_map/ppermute | solution.py:36
  101.6 81.5 %collective-permute-start.3 = (bf16[1,2,32,3584]{3,2,1,0:T(8,128)(2,1)}, bf16[1,2,32,3584]{3,2,1,0:T(8,128)(2,1)S(1)}, u32[]{:S(2)}, u32[]{:S(2)}) collective-permute-start(bf16[1,2,32,3584]{3,2,1,0:T(8,128)(2,1)} %copy-done.7), channel_id=1, source_target_pairs={{0,4},{2,6},{4,0},{6,2},{8,12},{10,14},{12,8},{14,10},{16,20},{18,... | collective-permute-start | bytes 1376264 | tf_op jit(solution)/shard_map/ppermute | solution.py:36
  126.5 27.6 %collective-permute-start.7 = (bf16[2,2,32,3584]{3,2,1,0:T(8,128)(2,1)}, bf16[2,2,32,3584]{3,2,1,0:T(8,128)(2,1)S(1)}, u32[]{:S(2)}, u32[]{:S(2)}) collective-permute-start(bf16[2,2,32,3584]{3,2,1,0:T(8,128)(2,1)} %collective-permute-done.6), channel_id=1, source_target_pairs={{8,16},{10,18},{12,20},{14,22},{16,24},{18,26},{20,28},{22,30},{9,... | collective-permute-start | bytes 2752520 | tf_op jit(solution)/shard_map/ppermute | solution.py:36
  135.1 20.5 %collective-permute-start.5 = (bf16[2,2,32,3584]{3,2,1,0:T(8,128)(2,1)}, bf16[2,2,32,3584]{3,2,1,0:T(8,128)(2,1)S(1)}, u32[]{:S(2)}, u32[]{:S(2)}) collective-permute-start(bf16[2,2,32,3584]{3,2,1,0:T(8,128)(2,1)} %collective-permute-done.4), channel_id=1, source_target_pairs={{8,0},{10,2},{12,4},{14,6},{16,8},{18,10},{20,12},{22,14},{9,1},{1... | collective-permute-start | bytes 2752520 | tf_op jit(solution)/shard_map/ppermute | solution.py:36
  138.8 41.8 %collective-permute-start.25 = (bf16[64,3584]{1,0:T(8,128)(2,1)S(1)}, bf16[64,3584]{1,0:T(8,128)(2,1)S(1)}, u32[]{:S(2)}, u32[]{:S(2)}) collective-permute-start(bf16[64,3584]{1,0:T(8,128)(2,1)S(1)} %get-tuple-element.19), channel_id=1, source_target_pairs={{0,1},{1,0},{2,3},{3,2},{4,5},{5,4},{6,7},{7,6},{8,9},{9,8},{10,11... | collective-permute-start | bytes 1376264 | tf_op jit(solution)/shard_map/ppermute | solution.py:36
  154.1 20.4 %collective-permute-start.10 = (bf16[2,2,32,3584]{3,2,1,0:T(8,128)(2,1)S(1)}, bf16[2,2,32,3584]{3,2,1,0:T(8,128)(2,1)S(1)}, u32[]{:S(2)}, u32[]{:S(2)}) collective-permute-start(bf16[2,2,32,3584]{3,2,1,0:T(8,128)(2,1)S(1)} %collective-permute-done.7), channel_id=1, source_target_pairs={{16,24},{18,26},{20,28},{22,30},{17,25},{19,27},{21,29},{23,31}} | collective-permute-start | bytes 2752520 | tf_op jit(solution)/shard_map/ppermute | solution.py:36
  155.8 23.8 %copy-start.2 = (bf16[2,2,32,3584]{3,2,1,0:T(8,128)(2,1)}, bf16[2,2,32,3584]{3,2,1,0:T(8,128)(2,1)S(1)}, u32[]{:S(2)}) copy-start(bf16[2,2,32,3584]{3,2,1,0:T(8,128)(2,1)S(1)} %broadcast_select_fusion.2.refs_3_) | copy-start | bytes 2752516
  155.8 27.3 %collective-permute-start.8 = (bf16[1,2,32,3584]{3,2,1,0:T(8,128)(2,1)S(1)}, bf16[1,2,32,3584]{3,2,1,0:T(8,128)(2,1)S(1)}, u32[]{:S(2)}, u32[]{:S(2)}) collective-permute-start(bf16[1,2,32,3584]{3,2,1,0:T(8,128)(2,1)S(1)} %get-tuple-element.49), channel_id=1, source_target_pairs={{0,2},{2,0},{4,6},{6,4},{8,10},{10,8},{12,14},{14,12},{16,18},{18,... | collective-permute-start | bytes 1376264 | tf_op jit(solution)/shard_map/ppermute | solution.py:36
  174.5 2.1 collective-permute-start.11
  176.6 13.5 %collective-permute-start.9 = (bf16[1,2,32,3584]{3,2,1,0:T(8,128)(2,1)S(1)}, bf16[1,2,32,3584]{3,2,1,0:T(8,128)(2,1)S(1)}, u32[]{:S(2)}, u32[]{:S(2)}) collective-permute-start(bf16[1,2,32,3584]{3,2,1,0:T(8,128)(2,1)S(1)} %get-tuple-element.48), channel_id=1, source_target_pairs={{0,4},{2,6},{4,0},{6,2},{8,12},{10,14},{12,8},{14,10},{16,20},{18,... | collective-permute-start | bytes 1376264 | tf_op jit(solution)/shard_map/ppermute | solution.py:36
  179.8 27.5 %collective-permute-start.13 = (bf16[2,2,32,3584]{3,2,1,0:T(8,128)(2,1)S(1)}, bf16[2,2,32,3584]{3,2,1,0:T(8,128)(2,1)S(1)}, u32[]{:S(2)}, u32[]{:S(2)}) collective-permute-start(bf16[2,2,32,3584]{3,2,1,0:T(8,128)(2,1)S(1)} %pad_maximum_fusion.2), channel_id=1, source_target_pairs={{0,4},{2,6},{4,0},{6,2},{8,12},{10,14},{12,8},{14,10},{16,20},{18,... | collective-permute-start | bytes 2752520 | tf_op jit(solution)/shard_map/ppermute | solution.py:36
  180.6 26.7 %collective-permute-start.12 = (bf16[2,2,32,3584]{3,2,1,0:T(8,128)(2,1)S(1)}, bf16[2,2,32,3584]{3,2,1,0:T(8,128)(2,1)}, u32[]{:S(2)}, u32[]{:S(2)}) collective-permute-start(bf16[2,2,32,3584]{3,2,1,0:T(8,128)(2,1)S(1)} %pad_maximum_fusion.1), channel_id=1, source_target_pairs={{0,2},{2,0},{4,6},{6,4},{8,10},{10,8},{12,14},{14,12},{16,18},{18,... | collective-permute-start | bytes 2752520 | tf_op jit(solution)/shard_map/ppermute | solution.py:36
  (14 other events, 63.4 us)

commit v2 on v1

--- a/solution.py
+++ b/solution.py
@@ -45,10 +45,7 @@
 
 
 def gather_groups(depth):
-    groups = {}
-    for k in range(depth):
-        groups.setdefault(max(k, depth - k) if k else 0, []).append(k)
-    return [groups[t] for t in sorted(groups)]
+    return [[k] for k in sorted(range(depth), key=lambda k: max(k, depth - k) if k else 0)]
 
 
 def reduce_groups(depth):
@@ -89,99 +86,113 @@
             out_specs=[pl.BlockSpec((rows // 2, tokens), lambda i, *_: (0, 0))] * 2,
             scratch_shapes=[pltpu.VMEM((rows, tokens), acts.dtype)],
         ),
+        compiler_params=pltpu.CompilerParams(vmem_limit_bytes=20 * 2**20),
         name="rows_by_owner",
     )(place, limit, acts)
 
 
-def hidden_kernel(groups, place, limit, *refs):
-    columns, out, full = refs[-3:]
+def hidden_kernel(offsets, depth, place, limit, *refs):
+    columns, out, full, ready, done = refs[-5:]
+    groups = [len(group) for group in offsets]
     upper, lower = lax.rem(place[0] // 2, 2), lax.rem(place[0], 2)
-    half = full.shape[1] // 8
-
-    def at(y, x, h):
-        return pl.ds(pl.multiple_of(((y * 2 + x) * 2 + h) * half, half), half)
-
-    start = 0
-    for size in groups:
-        far_a, far_b = refs[size : size + 2]
-        for m in range(size):
-            n = start + m
-            near = refs[m]
-
-            @pl.when((pl.program_id(0) == 0) & (pl.program_id(1) == n))
-            def _():
+    half = full.shape[0] // (8 * sum(groups))
+
+    def at(first, y, x, h):
+        return pl.ds(pl.multiple_of(first + ((y * 2 + x) * 2 + h) * half, half), half)
+
+    @pl.when(pl.program_id(0) == 0)
+    def _():
+        start, rest = 0, refs
+        for size in groups:
+            far_a, far_b = rest[size : size + 2]
+            for m in range(size):
+                first = (start + m) * 8 * half
                 for j in range(2):
                     y, x = upper ^ j, lower ^ j
-                    full[n, at(y, lower, 0)] = near[0, j]
-                    full[n, at(y, 1 - lower, 0)] = far_a[m, j]
-                    full[n, at(upper, x, 1)] = near[1, j]
-                    full[n, at(1 - upper, x, 1)] = far_b[m, j]
-
-        start += size
-        refs = refs[size + 2 :]
+                    full[at(first, y, lower, 0)] = rest[m][0, j]
+                    full[at(first, y, 1 - lower, 0)] = far_a[m, j]
+                    full[at(first, upper, x, 1)] = rest[m][1, j]
+                    full[at(first, 1 - upper, x, 1)] = far_b[m, j]
+            start += size
+            rest = rest[size + 2 :]
 
     product = lax.dot_general(
-        columns[...],
-        full[pl.program_id(1)],
-        (((1,), (1,)), ((), ())),
-        preferred_element_type=jnp.float32,
+        columns[...], full[...], (((1,), (1,)), ((), ())), preferred_element_type=jnp.float32
     )
     product = columns.shape[1] ** (-0.5) * product
-    first = pl.program_id(0) * product.shape[0]
-    token = first + lax.broadcasted_iota(jnp.int32, product.shape, 0)
-    out[...] = jnp.where(token < limit[0], product, 0.0).astype(out.dtype)
+    height = product.shape[0]
+    step = pl.program_id(0)
+    token = step * height + lax.broadcasted_iota(jnp.int32, product.shape, 0)
+    ready[step] = jnp.where(token < limit[0], product, 0.0).astype(ready.dtype)
+
+    def copies(t):
+        found = []
+        for n, k in enumerate(k for group in offsets for k in group):
+            slot = lax.rem(place[0] // 4 + k, depth)
+            found.append(
+                pltpu.make_async_copy(
+                    ready.at[t, :, pl.ds(n * 8 * half, 8 * half)],
+                    out.at[
+                        pl.ds(pl.multiple_of(t * height, height), height),
+                        pl.ds(pl.multiple_of(slot * 8 * half, 8 * half), 8 * half),
+                    ],
+                    done.at[t, n],
+                )
+            )
+        return found
+
+    for copy in copies(step):
+        copy.start()
+
+    @pl.when(step == pl.num_programs(0) - 1)
+    def _():
+        for t in range(ready.shape[0]):
+            for copy in copies(t):
+                copy.wait()
 
 
 def hidden_columns(place, limit, groups, columns, so_far, depth):
     tokens, width = columns.shape
-    offsets = [k for group, _ in groups for k in group]
+    offsets = [group for group, _ in groups]
+    blocks = sum(len(group) for group in offsets)
     block = 8 * groups[0][1][0].shape[2]
     steps = 2
 
-    def slot(place, k):
-        return lax.rem(place[0] // 4 + k, depth)
-
     def same(array):
         zeros = (0,) * array.ndim
-        return pl.BlockSpec(array.shape, lambda t, n, *_: zeros, pipeline_mode=pl.Buffered(1))
-
-    in_specs, args = [], [place, limit]
-    for _, arrays in groups:
-        in_specs += [same(array) for array in arrays]
-        args += arrays
-    in_specs.append(pl.BlockSpec((tokens // steps, width), lambda t, n, *_: (t, 0)))
-    args.append(columns)
-    aliases = {}
-    kernel = functools.partial(hidden_kernel, [len(group) for group, _ in groups])
+        return pl.BlockSpec(array.shape, lambda t, *_: zeros, pipeline_mode=pl.Buffered(1))
+
+    args = [place, limit] + [array for _, arrays in groups for array in arrays] + [columns]
+    in_specs = [same(array) for array in args[2:-1]]
+    in_specs.append(pl.BlockSpec((tokens // steps, width), lambda t, *_: (t, 0)))
+    kernel, aliases = functools.partial(hidden_kernel, offsets, depth), {}
     if so_far is not None:
         in_specs.insert(0, pl.BlockSpec(memory_space=pl.ANY))
         args.insert(2, so_far)
         aliases = {2: 0}
         inner = kernel
         kernel = lambda place, limit, so_far, *refs: inner(place, limit, *refs)
-
-    def target(t, n, place, limit):
-        at = slot(place, offsets[0])
-        for m, k in enumerate(offsets[1:], 1):
-            at = jnp.where(n == m, slot(place, k), at)
-        return t, at
-
     return pl.pallas_call(
         kernel,
         out_shape=jax.ShapeDtypeStruct((tokens, depth * block), jnp.bfloat16),
         grid_spec=pltpu.PrefetchScalarGridSpec(
             num_scalar_prefetch=2,
-            grid=(steps, len(offsets)),
+            grid=(steps,),
             in_specs=in_specs,
-            out_specs=pl.BlockSpec((tokens // steps, block), target),
-            scratch_shapes=[pltpu.VMEM((len(offsets), block, width), jnp.bfloat16)],
+            out_specs=pl.BlockSpec(memory_space=pl.ANY),
+            scratch_shapes=[
+                pltpu.VMEM((blocks * block, width), jnp.bfloat16),
+                pltpu.VMEM((steps, tokens // steps, blocks * block), jnp.bfloat16),
+                pltpu.SemaphoreType.DMA((steps, blocks)),
+            ],
         ),
         input_output_aliases=aliases,
         cost_estimate=pl.CostEstimate(
-            flops=2 * tokens * width * block * len(offsets),
+            flops=2 * tokens * width * block * blocks,
             transcendentals=0,
             bytes_accessed=2 * tokens * width,
         ),
+        compiler_params=pltpu.CompilerParams(vmem_limit_bytes=24 * 2**20),
         name="hidden_columns",
     )(*args)
 
@@ -216,8 +227,9 @@
         up = below[t] = move(up, pairs_along(count, 1, t - 1, depth - 1))
         down = above[t] = move(down, pairs_along(count, -1, 1, depth - t + 1))
     near = {0: base}
-    for k in range(1, depth):
-        near[k] = jnp.where(outer + k < depth, above[k], below[depth - k])
+    for g, group in enumerate(gather_groups(depth)[1:], 1):
+        for k in group:
+            near[k] = jnp.where(outer + k < depth, above[k], below[depth - k])
     gathered = []
     for group in gather_groups(depth):
         far_a = move(jnp.stack([near[k][0] for k in group]), across_x)
@@ -306,11 +318,12 @@
         source = lax.rem(mine + groups - shift, groups)
         incoming = jnp.where(wanted == source, other[None], incoming)
     served = serving[0].astype(jnp.float32) + incoming.astype(jnp.float32)
+    served = served.astype(jnp.bfloat16)
 
     if by_kernel:
         d_hid = None
-        for some in (gathered[:-1], gathered[-1:]):
-            d_hid = hidden_columns(place, limit, some, grads_out, d_hid, depth)
+        for some in gathered:
+            d_hid = hidden_columns(place, limit, [some], grads_out, d_hid, depth)
     else:
         blocks = {}
         for group, arrays in gathered:
@@ -331,7 +344,7 @@
         updated.astype(jnp.bfloat16)[None],
         first_new[None],
         squares_new[None],
-        served.astype(jnp.bfloat16)[None],
+        served[None],
     )
 
 

time: 218 us -> 206 us (0.945)
  the two profiles are of different devices: /device:TPU:16 before, /device:TPU:0 now
where the time goes in v2:
time: 206 us
  waiting for transfers between devices  126 us (61%)
  starting transfers between devices  35.3 us (17%)
  Pallas kernels  13.5 us (7%)
  matrix products  11.6 us (6%)
  other arithmetic  11.5 us (6%)
  local copies, waits for them, and re-layouts  5.71 us (3%)
    ppermute x28, waiting for transfers between devices, move(): return lax.ppermute(value, axis, pairs)  126 us
    ppermute x28, starting transfers between devices, move(): return lax.ppermute(value, axis, pairs)  35.3 us
    pallas_call x4, Pallas kernels, hidden_columns(): pl.pallas_call(kernel, out_shape=jax.ShapeDtypeStruct((tokens, depth * bl...  12.7 us
    dot_general x3, matrix products, term(): product = jnp.dot(picked, grads_out, preferred_element_type=jnp.float32)  11.6 us
    unnamed x22, local copies, waits for them, and re-layouts  4.71 us
  transfers between devices with their start and end apart: 28, of which 11 were waited for; matrix products, arithmetic and copies ran while one was open for 9% of the time, Pallas kernels for 5%

profile of v2, /device:TPU:0, one launch (start us, length us, event | category | flops | bytes accessed | tf_op | source)
XLA Modules:
  0.0 205.7 jit_solution(16482457037036928086)
XLA Ops:
  1.3 1.6 copy-done.1
  3.7 5.6 %fusion.1 = f16[256,3584]{1,0:T(8,128)(2,1)S(1)} fusion(bf16[512,1024]{1,0:T(8,128)(2,1)S(1)} %get-tuple-element.13, bf16[1,1024,3584]{2,1,0:T(8,128)(2,1)} %param.9), kind=kOutput, calls=%fused_computation.4 | convolution fusion | flops 1880883200 | bytes 9699328 | tf_op jit(solution)/shard_map/dot_general | solution.py:259
  9.5 3.0 %collective-permute-start.17 = (f16[2,2,32,3584]{3,2,1,0:T(8,128)(2,1)S(1)}, f16[2,2,32,3584]{3,2,1,0:T(8,128)(2,1)S(1)}, u32[]{:S(2)}, u32[]{:S(2)}) collective-permute-start(f16[2,2,32,3584]{3,2,1,0:T(8,128)(2,1)S(1)} %bitcast.242), channel_id=1, source_target_pairs={{0,2},{2,0},{4,6},{6,4},{8,10},{10,8},{12,14},{14,12},{16,18},{18,... | collective-permute-start | bytes 2752520 | tf_op jit(solution)/shard_map/ppermute | solution.py:36
  12.6 1.5 collective-permute-start.18
  14.1 2.1 %fusion = f16[256,3584]{1,0:T(8,128)(2,1)S(1)} fusion(bf16[512,1024]{1,0:T(8,128)(2,1)S(1)} %get-tuple-element.13, bf16[1,1024,3584]{2,1,0:T(8,128)(2,1)S(1)} %bitcast.226), kind=kOutput, calls=%fused_computation.3 | convolution fusion | flops 1880883200 | bytes 9699328 | tf_op jit(solution)/shard_map/dot_general | solution.py:259
  17.4 2.0 collective-permute-start
  19.4 4.0 %convolution_multiply_fusion = f32[512,3584]{1,0:T(8,128)S(1)} fusion(bf16[512,1024]{1,0:T(8,128)(2,1)S(1)} %get-tuple-element.12, bf16[1,1024,3584]{2,1,0:T(8,128)(2,1)S(1)} %bitcast.226), kind=kOutput, calls=%fused_computation | convolution fusion | flops 3759931392 | bytes 15728640 | tf_op jit(solution)/shard_map/dot_general | solution.py:259
  23.4 35.6 %collective-permute-done = bf16[32,3584]{1,0:T(8,128)(2,1)S(1)} collective-permute-done((bf16[32,3584]{1,0:T(8,128)(2,1)S(1)}, bf16[32,3584]{1,0:T(8,128)(2,1)S(1)}, u32[]{:S(2)}, u32[]{:S(2)}) %collective-permute-start) | collective-permute-done | bytes 229408 | tf_op jit(solution)/shard_map/ppermute | solution.py:36
  59.4 5.8 %collective-permute-done.1 = bf16[32,3584]{1,0:T(8,128)(2,1)S(1)} collective-permute-done((bf16[32,3584]{1,0:T(8,128)(2,1)S(1)}, bf16[32,3584]{1,0:T(8,128)(2,1)S(1)}, u32[]{:S(2)}, u32[]{:S(2)}) %collective-permute-start.1) | collective-permute-done | bytes 229408 | tf_op jit(solution)/shard_map/ppermute | solution.py:36
  66.6 5.5 %collective-permute-start.6 = (bf16[2,2,32,3584]{3,2,1,0:T(8,128)(2,1)S(1)}, bf16[2,2,32,3584]{3,2,1,0:T(8,128)(2,1)}, u32[]{:S(2)}, u32[]{:S(2)}) collective-permute-start(bf16[2,2,32,3584]{3,2,1,0:T(8,128)(2,1)S(1)} %pad_maximum_fusion.refs_0_), channel_id=1, source_target_pairs={{0,8},{2,10},{4,12},{6,14},{8,16},{10,18},{12,20},{14,22},{16,24},... | collective-permute-start | bytes 2752520 | tf_op jit(solution)/shard_map/ppermute | solution.py:36
  74.4 1.5 collective-permute-start.20
  76.2 16.5 %collective-permute-done.22 = f16[2,32,3584]{2,1,0:T(8,128)(2,1)S(1)} collective-permute-done((f16[2,32,3584]{2,1,0:T(8,128)(2,1)S(1)}, f16[2,32,3584]{2,1,0:T(8,128)(2,1)S(1)}, u32[]{:S(2)}, u32[]{:S(2)}) %collective-permute-start.22) | collective-permute-done | bytes 458784 | tf_op jit(solution)/shard_map/ppermute | solution.py:36
  96.9 4.6 %collective-permute-done.23 = f16[2,32,3584]{2,1,0:T(8,128)(2,1)S(1)} collective-permute-done((f16[2,32,3584]{2,1,0:T(8,128)(2,1)S(1)}, f16[2,32,3584]{2,1,0:T(8,128)(2,1)S(1)}, u32[]{:S(2)}, u32[]{:S(2)}) %collective-permute-start.23) | collective-permute-done | bytes 458784 | tf_op jit(solution)/shard_map/ppermute | solution.py:36
  101.5 1.5 collective-permute-start.3
  103.8 2.1 %collective-permute-start.25 = (f16[64,3584]{1,0:T(8,128)(2,1)}, f16[64,3584]{1,0:T(8,128)(2,1)}, u32[]{:S(2)}, u32[]{:S(2)}) collective-permute-start(f16[64,3584]{1,0:T(8,128)(2,1)} %pad_maximum_fusion.2), channel_id=1, source_target_pairs={{16,0},{18,2},{20,4},{22,6},{24,8},{26,10},{28,12},{30,14},{0,16},... | collective-permute-start | bytes 1376264 | tf_op jit(solution)/shard_map/ppermute | solution.py:36
  107.7 3.9 %collective-permute-done.3.refs_2_ = bf16[1,2,32,3584]{3,2,1,0:T(8,128)(2,1)S(1)} collective-permute-done((bf16[1,2,32,3584]{3,2,1,0:T(8,128)(2,1)S(1)}, bf16[1,2,32,3584]{3,2,1,0:T(8,128)(2,1)S(1)}, u32[]{:S(2)}, u32[]{:S(2)}) %collective-permute-start.3) | collective-permute-done | bytes 458784 | tf_op jit(solution)/shard_map/ppermute | solution.py:36
  112.1 3.1 %copy-done = bf16[1,1024,3584]{2,1,0:T(8,128)(2,1)S(1)} copy-done((bf16[1,1024,3584]{2,1,0:T(8,128)(2,1)S(1)}, bf16[1,1024,3584]{2,1,0:T(8,128)(2,1)}, u32[]{:S(2)}) %copy-start) | copy-done | bytes 7340056
  115.2 3.2 %hidden_columns.4.so_far = bf16[1024,1024]{1,0:T(8,128)(2,1)} custom-call(s32[1]{0:T(128)} %bitcast.place, s32[1]{0:T(128)} %bitcast.220.limit, bf16[2,2,32,3584]{3,2,1,0:T(8,128)(2,1)S(1)} %pad_maximum_fusion.refs_0_, bf16[1,2,32,3584]{3,2,1,0:T(8,128)(2,1)S(1)} %collective-permute-done.2.refs_1_, ...), custom_call_target="tpu_custom_call" | custom-call | flops 1879048192 | bytes 7340032 | tf_op jit(solution)/shard_map/hidden_columns/pallas_call | solution.py:175
  120.6 16.2 %collective-permute-done.26 = f16[64,3584]{1,0:T(8,128)(2,1)} collective-permute-done((f16[64,3584]{1,0:T(8,128)(2,1)}, f16[64,3584]{1,0:T(8,128)(2,1)}, u32[]{:S(2)}, u32[]{:S(2)}) %collective-permute-start.26) | collective-permute-done | bytes 458784 | tf_op jit(solution)/shard_map/ppermute | solution.py:36
  136.8 2.3 %fusion.4 = (bf16[64,3584]{1,0:T(8,128)(2,1)S(1)}, bf16[64,3584]{1,0:T(8,128)(2,1)S(1)}, f32[64,3584]{1,0:T(8,128)S(1)}) fusion(bf16[1,64,3584]{2,1,0:T(8,128)(2,1)S(1)} %copy-done.4, f32[1,64,3584]{2,1,0:T(8,128)S(1)} %copy-done.2, f32[1,64,3584]{2,1,0:T(8,128)S(1)} %copy-done.3, f16[64,3584]{1,0:T(8,128)(2,1)} %collective-permute-done.26, ...), kind=kLoop, calls=%fused_computation.11 | loop fusion | flops 6193152 | bytes 6422528 | tf_op jit(solution)/shard_map/convert_element_type | solution.py:309
  139.2 1.5 fusion.38
  141.5 12.4 %collective-permute-done.5 = bf16[2,2,32,3584]{3,2,1,0:T(8,128)(2,1)S(1)} collective-permute-done((bf16[2,2,32,3584]{3,2,1,0:T(8,128)(2,1)}, bf16[2,2,32,3584]{3,2,1,0:T(8,128)(2,1)S(1)}, u32[]{:S(2)}, u32[]{:S(2)}) %collective-permute-start.5) | collective-permute-done | bytes 917536 | tf_op jit(solution)/shard_map/ppermute | solution.py:36
  156.5 1.5 broadcast_select_fusion.1.refs_0_
  159.5 23.1 %collective-permute-done.13 = bf16[2,2,32,3584]{3,2,1,0:T(8,128)(2,1)S(1)} collective-permute-done((bf16[2,2,32,3584]{3,2,1,0:T(8,128)(2,1)S(1)}, bf16[2,2,32,3584]{3,2,1,0:T(8,128)(2,1)S(1)}, u32[]{:S(2)}, u32[]{:S(2)}) %collective-permute-start.13) | collective-permute-done | bytes 917536 | tf_op jit(solution)/shard_map/ppermute | solution.py:36
  182.7 1.7 collective-permute-start.12
  184.6 1.7 collective-permute-start.14
  186.6 1.9 add_convert_fusion
  188.5 3.2 %hidden_columns.5.so_far = bf16[1024,1024]{1,0:T(8,128)(2,1)} custom-call(s32[1]{0:T(128)} %bitcast.place, s32[1]{0:T(128)} %bitcast.221.limit, bf16[1024,1024]{1,0:T(8,128)(2,1)} %hidden_columns.4.so_far, bf16[2,2,32,3584]{3,2,1,0:T(8,128)(2,1)S(1)} %broadcast_select_fusion.2.refs_0_, ...), custom_call_target="tpu_custom_call", output_to_operand_aliasing={{}: (2, {})} | custom-call | flops 1879048192 | bytes 7340032 | tf_op jit(solution)/shard_map/hidden_columns/pallas_call | solution.py:175
  191.7 4.3 %collective-permute-done.12.refs_2_ = bf16[1,2,32,3584]{3,2,1,0:T(8,128)(2,1)S(1)} collective-permute-done((bf16[1,2,32,3584]{3,2,1,0:T(8,128)(2,1)S(1)}, bf16[1,2,32,3584]{3,2,1,0:T(8,128)(2,1)S(1)}, u32[]{:S(2)}, u32[]{:S(2)}) %collective-permute-start.12) | collective-permute-done | bytes 458784 | tf_op jit(solution)/shard_map/ppermute | solution.py:36
  196.1 3.2 %hidden_columns.6.so_far = bf16[1024,1024]{1,0:T(8,128)(2,1)} custom-call(s32[1]{0:T(128)} %bitcast.place, s32[1]{0:T(128)} %bitcast.222.limit, bf16[1024,1024]{1,0:T(8,128)(2,1)} %hidden_columns.5.so_far, bf16[2,2,32,3584]{3,2,1,0:T(8,128)(2,1)S(1)} %broadcast_select_fusion.1.refs_0_, ...), custom_call_target="tpu_custom_call", output_to_operand_aliasing={{}: (2, {})} | custom-call | flops 1879048192 | bytes 7340032 | tf_op jit(solution)/shard_map/hidden_columns/pallas_call | solution.py:175
  199.2 3.1 %collective-permute-done.15.refs_2_ = bf16[1,2,32,3584]{3,2,1,0:T(8,128)(2,1)S(1)} collective-permute-done((bf16[1,2,32,3584]{3,2,1,0:T(8,128)(2,1)S(1)}, bf16[1,2,32,3584]{3,2,1,0:T(8,128)(2,1)S(1)}, u32[]{:S(2)}, u32[]{:S(2)}) %collective-permute-start.15) | collective-permute-done | bytes 458784 | tf_op jit(solution)/shard_map/ppermute | solution.py:36
  202.3 3.2 %hidden_columns.7 = bf16[1024,1024]{1,0:T(8,128)(2,1)} custom-call(s32[1]{0:T(128)} %bitcast.place, s32[1]{0:T(128)} %bitcast.223.limit, bf16[1024,1024]{1,0:T(8,128)(2,1)} %hidden_columns.6.so_far, bf16[2,2,32,3584]{3,2,1,0:T(8,128)(2,1)S(1)} %broadcast_select_fusion.refs_0_, ...), custom_call_target="tpu_custom_call", output_to_operand_aliasing={{}: (2, {})} | custom-call | flops 1879048192 | bytes 7340032 | tf_op jit(solution)/shard_map/hidden_columns/pallas_call | solution.py:175
  (80 shorter events, 21.6 us)
Async XLA Ops:
  9.5 57.1 %collective-permute-start.17 = (f16[2,2,32,3584]{3,2,1,0:T(8,128)(2,1)S(1)}, f16[2,2,32,3584]{3,2,1,0:T(8,128)(2,1)S(1)}, u32[]{:S(2)}, u32[]{:S(2)}) collective-permute-start(f16[2,2,32,3584]{3,2,1,0:T(8,128)(2,1)S(1)} %bitcast.242), channel_id=1, source_target_pairs={{0,2},{2,0},{4,6},{6,4},{8,10},{10,8},{12,14},{14,12},{16,18},{18,... | collective-permute-start | bytes 2752520 | tf_op jit(solution)/shard_map/ppermute | solution.py:36
  12.6 59.5 %collective-permute-start.18 = (f16[2,2,32,3584]{3,2,1,0:T(8,128)(2,1)S(1)}, f16[2,2,32,3584]{3,2,1,0:T(8,128)(2,1)S(1)}, u32[]{:S(2)}, u32[]{:S(2)}) collective-permute-start(f16[2,2,32,3584]{3,2,1,0:T(8,128)(2,1)S(1)} %bitcast.241), channel_id=1, source_target_pairs={{0,4},{2,6},{4,0},{6,2},{8,12},{10,14},{12,8},{14,10},{16,20},{18,... | collective-permute-start | bytes 2752520 | tf_op jit(solution)/shard_map/ppermute | solution.py:36
  16.7 56.3 %collective-permute-start.21 = (f16[2,2,32,3584]{3,2,0,1:T(8,128)(2,1)S(1)}, f16[2,2,32,3584]{3,2,0,1:T(8,128)(2,1)S(1)}, u32[]{:S(2)}, u32[]{:S(2)}) collective-permute-start(f16[2,2,32,3584]{3,2,0,1:T(8,128)(2,1)S(1)} %copy.18), channel_id=1, source_target_pairs={{0,4},{2,6},{4,0},{6,2},{8,12},{10,14},{12,8},{14,10},{16,20},{18,... | collective-permute-start | bytes 2752520 | tf_op jit(solution)/shard_map/ppermute | solution.py:36
  17.2 57.2 %collective-permute-start.16 = (f16[2,2,32,3584]{3,2,1,0:T(8,128)(2,1)S(1)}, f16[2,2,32,3584]{3,2,1,0:T(8,128)(2,1)S(1)}, u32[]{:S(2)}, u32[]{:S(2)}) collective-permute-start(f16[2,2,32,3584]{3,2,1,0:T(8,128)(2,1)S(1)} %bitcast.240), channel_id=1, source_target_pairs={{0,2},{2,0},{4,6},{6,4},{8,10},{10,8},{12,14},{14,12},{16,18},{18,... | collective-permute-start | bytes 2752520 | tf_op jit(solution)/shard_map/ppermute | solution.py:36
  17.4 41.6 %collective-permute-start = (bf16[32,3584]{1,0:T(8,128)(2,1)S(1)}, bf16[32,3584]{1,0:T(8,128)(2,1)S(1)}, u32[]{:S(2)}, u32[]{:S(2)}) collective-permute-start(bf16[32,3584]{1,0:T(8,128)(2,1)S(1)} %get-tuple-element.52), channel_id=1, source_target_pairs={{0,4},{2,6},{4,0},{6,2},{8,12},{10,14},{12,8},{14,10},{16,20},{18,... | collective-permute-start | bytes 688136 | tf_op jit(solution)/shard_map/ppermute | solution.py:36
  59.0 6.2 %collective-permute-start.1 = (bf16[32,3584]{1,0:T(8,128)(2,1)S(1)}, bf16[32,3584]{1,0:T(8,128)(2,1)S(1)}, u32[]{:S(2)}, u32[]{:S(2)}) collective-permute-start(bf16[32,3584]{1,0:T(8,128)(2,1)S(1)} %get-tuple-element.51), channel_id=1, source_target_pairs={{0,2},{2,0},{4,6},{6,4},{8,10},{10,8},{12,14},{14,12},{16,18},{18,... | collective-permute-start | bytes 688136 | tf_op jit(solution)/shard_map/ppermute | solution.py:36
  65.3 53.1 %collective-permute-start.4 = (bf16[2,2,32,3584]{3,2,1,0:T(8,128)(2,1)S(1)}, bf16[2,2,32,3584]{3,2,1,0:T(8,128)(2,1)}, u32[]{:S(2)}, u32[]{:S(2)}) collective-permute-start(bf16[2,2,32,3584]{3,2,1,0:T(8,128)(2,1)S(1)} %pad_maximum_fusion.refs_0_), channel_id=1, source_target_pairs={{8,0},{10,2},{12,4},{14,6},{16,8},{18,10},{20,12},{22,14},{24,16},... | collective-permute-start | bytes 2752520 | tf_op jit(solution)/shard_map/ppermute | solution.py:36
  66.6 53.1 %collective-permute-start.6 = (bf16[2,2,32,3584]{3,2,1,0:T(8,128)(2,1)S(1)}, bf16[2,2,32,3584]{3,2,1,0:T(8,128)(2,1)}, u32[]{:S(2)}, u32[]{:S(2)}) collective-permute-start(bf16[2,2,32,3584]{3,2,1,0:T(8,128)(2,1)S(1)} %pad_maximum_fusion.refs_0_), channel_id=1, source_target_pairs={{0,8},{2,10},{4,12},{6,14},{8,16},{10,18},{12,20},{14,22},{16,24},... | collective-permute-start | bytes 2752520 | tf_op jit(solution)/shard_map/ppermute | solution.py:36
  72.1 35.2 %collective-permute-start.2 = (bf16[1,2,32,3584]{3,2,1,0:T(8,128)(2,1)S(1)}, bf16[1,2,32,3584]{3,2,1,0:T(8,128)(2,1)S(1)}, u32[]{:S(2)}, u32[]{:S(2)}) collective-permute-start(bf16[1,2,32,3584]{3,2,1,0:T(8,128)(2,1)S(1)} %maximum_bitcast_fusion), channel_id=1, source_target_pairs={{0,2},{2,0},{4,6},{6,4},{8,10},{10,8},{12,14},{14,12},{16,18},{18,... | collective-permute-start | bytes 1376264 | tf_op jit(solution)/shard_map/ppermute | solution.py:36
  73.0 19.6 %collective-permute-start.22 = (f16[2,32,3584]{2,1,0:T(8,128)(2,1)S(1)}, f16[2,32,3584]{2,1,0:T(8,128)(2,1)S(1)}, u32[]{:S(2)}, u32[]{:S(2)}) collective-permute-start(f16[2,32,3584]{2,1,0:T(8,128)(2,1)S(1)} %get-tuple-element.36), channel_id=1, source_target_pairs={{0,2},{2,0},{4,6},{6,4},{8,10},{10,8},{12,14},{14,12},{16,18},{18,... | collective-permute-start | bytes 1376264 | tf_op jit(solution)/shard_map/ppermute | solution.py:36
  74.4 18.8 %collective-permute-start.20 = (f16[2,32,3584]{2,1,0:T(8,128)(2,1)S(1)}, f16[2,32,3584]{2,1,0:T(8,128)(2,1)S(1)}, u32[]{:S(2)}, u32[]{:S(2)}) collective-permute-start(f16[2,32,3584]{2,1,0:T(8,128)(2,1)S(1)} %get-tuple-element.37), channel_id=1, source_target_pairs={{0,4},{2,6},{4,0},{6,2},{8,12},{10,14},{12,8},{14,10},{16,20},{18,... | collective-permute-start | bytes 1376264 | tf_op jit(solution)/shard_map/ppermute | solution.py:36
  92.6 8.9 %collective-permute-start.23 = (f16[2,32,3584]{2,1,0:T(8,128)(2,1)S(1)}, f16[2,32,3584]{2,1,0:T(8,128)(2,1)S(1)}, u32[]{:S(2)}, u32[]{:S(2)}) collective-permute-start(f16[2,32,3584]{2,1,0:T(8,128)(2,1)S(1)} %get-tuple-element.35), channel_id=1, source_target_pairs={{0,2},{2,0},{4,6},{6,4},{8,10},{10,8},{12,14},{14,12},{16,18},{18,... | collective-permute-start | bytes 1376264 | tf_op jit(solution)/shard_map/ppermute | solution.py:36
  93.3 10.6 %collective-permute-start.19 = (f16[2,32,3584]{2,1,0:T(8,128)(2,1)S(1)}, f16[2,32,3584]{2,1,0:T(8,128)(2,1)S(1)}, u32[]{:S(2)}, u32[]{:S(2)}) collective-permute-start(f16[2,32,3584]{2,1,0:T(8,128)(2,1)S(1)} %get-tuple-element.34), channel_id=1, source_target_pairs={{0,4},{2,6},{4,0},{6,2},{8,12},{10,14},{12,8},{14,10},{16,20},{18,... | collective-permute-start | bytes 1376264 | tf_op jit(solution)/shard_map/ppermute | solution.py:36
  101.5 10.1 %collective-permute-start.3 = (bf16[1,2,32,3584]{3,2,1,0:T(8,128)(2,1)S(1)}, bf16[1,2,32,3584]{3,2,1,0:T(8,128)(2,1)S(1)}, u32[]{:S(2)}, u32[]{:S(2)}) collective-permute-start(bf16[1,2,32,3584]{3,2,1,0:T(8,128)(2,1)S(1)} %maximum_bitcast_fusion.1), channel_id=1, source_target_pairs={{0,4},{2,6},{4,0},{6,2},{8,12},{10,14},{12,8},{14,10},{16,20},{18,... | collective-permute-start | bytes 1376264 | tf_op jit(solution)/shard_map/ppermute | solution.py:36
  103.8 33.0 %collective-permute-start.25 = (f16[64,3584]{1,0:T(8,128)(2,1)}, f16[64,3584]{1,0:T(8,128)(2,1)}, u32[]{:S(2)}, u32[]{:S(2)}) collective-permute-start(f16[64,3584]{1,0:T(8,128)(2,1)} %pad_maximum_fusion.2), channel_id=1, source_target_pairs={{16,0},{18,2},{20,4},{22,6},{24,8},{26,10},{28,12},{30,14},{0,16},... | collective-permute-start | bytes 1376264 | tf_op jit(solution)/shard_map/ppermute | solution.py:36
  107.3 29.6 %collective-permute-start.26 = (f16[64,3584]{1,0:T(8,128)(2,1)}, f16[64,3584]{1,0:T(8,128)(2,1)}, u32[]{:S(2)}, u32[]{:S(2)}) collective-permute-start(f16[64,3584]{1,0:T(8,128)(2,1)} %pad_maximum_fusion.3), channel_id=1, source_target_pairs={{8,0},{10,2},{12,4},{14,6},{16,8},{18,10},{20,12},{22,14},{24,16},... | collective-permute-start | bytes 1376264 | tf_op jit(solution)/shard_map/ppermute | solution.py:36
  111.6 25.2 %collective-permute-start.24 = (f16[64,3584]{1,0:T(8,128)(2,1)}, f16[64,3584]{1,0:T(8,128)(2,1)}, u32[]{:S(2)}, u32[]{:S(2)}) collective-permute-start(f16[64,3584]{1,0:T(8,128)(2,1)} %pad_maximum_fusion.1), channel_id=1, source_target_pairs={{24,0},{26,2},{28,4},{30,6},{0,8},{2,10},{4,12},{6,14},{8,16},{10,... | collective-permute-start | bytes 1376264 | tf_op jit(solution)/shard_map/ppermute | solution.py:36
  115.2 21.6 %copy-start.2 = (f32[1,64,3584]{2,1,0:T(8,128)S(1)}, f32[1,64,3584]{2,1,0:T(8,128)}, u32[]{:S(2)}) copy-start(f32[1,64,3584]{2,1,0:T(8,128)} %param.14) | copy-start | bytes 2752516
  115.2 21.6 %copy-start.3 = (f32[1,64,3584]{2,1,0:T(8,128)S(1)}, f32[1,64,3584]{2,1,0:T(8,128)}, u32[]{:S(2)}) copy-start(f32[1,64,3584]{2,1,0:T(8,128)} %param.13) | copy-start | bytes 2752516
  118.4 35.5 %collective-permute-start.5 = (bf16[2,2,32,3584]{3,2,1,0:T(8,128)(2,1)}, bf16[2,2,32,3584]{3,2,1,0:T(8,128)(2,1)S(1)}, u32[]{:S(2)}, u32[]{:S(2)}) collective-permute-start(bf16[2,2,32,3584]{3,2,1,0:T(8,128)(2,1)} %collective-permute-done.4), channel_id=1, source_target_pairs={{8,0},{10,2},{12,4},{14,6},{16,8},{18,10},{20,12},{22,14},{9,1},{1... | collective-permute-start | bytes 2752520 | tf_op jit(solution)/shard_map/ppermute | solution.py:36
  119.7 21.1 %collective-permute-start.7 = (bf16[2,2,32,3584]{3,2,1,0:T(8,128)(2,1)}, bf16[2,2,32,3584]{3,2,1,0:T(8,128)(2,1)S(1)}, u32[]{:S(2)}, u32[]{:S(2)}) collective-permute-start(bf16[2,2,32,3584]{3,2,1,0:T(8,128)(2,1)} %collective-permute-done.6), channel_id=1, source_target_pairs={{8,16},{10,18},{12,20},{14,22},{16,24},{18,26},{20,28},{22,30},{9,... | collective-permute-start | bytes 2752520 | tf_op jit(solution)/shard_map/ppermute | solution.py:36
  139.1 45.4 %collective-permute-start.27 = (bf16[64,3584]{1,0:T(8,128)(2,1)S(1)}, bf16[64,3584]{1,0:T(8,128)(2,1)S(1)}, u32[]{:S(2)}, u32[]{:S(2)}) collective-permute-start(bf16[64,3584]{1,0:T(8,128)(2,1)S(1)} %get-tuple-element.19), channel_id=1, source_target_pairs={{0,1},{1,0},{2,3},{3,2},{4,5},{5,4},{6,7},{7,6},{8,9},{9,8},{10,11... | collective-permute-start | bytes 1376264 | tf_op jit(solution)/shard_map/ppermute | solution.py:36
  140.8 15.8 %collective-permute-start.10 = (bf16[2,2,32,3584]{3,2,1,0:T(8,128)(2,1)S(1)}, bf16[2,2,32,3584]{3,2,1,0:T(8,128)(2,1)S(1)}, u32[]{:S(2)}, u32[]{:S(2)}) collective-permute-start(bf16[2,2,32,3584]{3,2,1,0:T(8,128)(2,1)S(1)} %collective-permute-done.7), channel_id=1, source_target_pairs={{16,24},{18,26},{20,28},{22,30},{17,25},{19,27},{21,29},{23,31}} | collective-permute-start | bytes 2752520 | tf_op jit(solution)/shard_map/ppermute | solution.py:36
  154.0 32.3 %collective-permute-start.8 = (bf16[1,2,32,3584]{3,2,1,0:T(8,128)(2,1)S(1)}, bf16[1,2,32,3584]{3,2,1,0:T(8,128)(2,1)S(1)}, u32[]{:S(2)}, u32[]{:S(2)}) collective-permute-start(bf16[1,2,32,3584]{3,2,1,0:T(8,128)(2,1)S(1)} %get-tuple-element.49), channel_id=1, source_target_pairs={{0,2},{2,0},{4,6},{6,4},{8,10},{10,8},{12,14},{14,12},{16,18},{18,... | collective-permute-start | bytes 1376264 | tf_op jit(solution)/shard_map/ppermute | solution.py:36
  154.7 33.9 %collective-permute-start.9 = (bf16[1,2,32,3584]{3,2,1,0:T(8,128)(2,1)S(1)}, bf16[1,2,32,3584]{3,2,1,0:T(8,128)(2,1)S(1)}, u32[]{:S(2)}, u32[]{:S(2)}) collective-permute-start(bf16[1,2,32,3584]{3,2,1,0:T(8,128)(2,1)S(1)} %get-tuple-element.48), channel_id=1, source_target_pairs={{0,4},{2,6},{4,0},{6,2},{8,12},{10,14},{12,8},{14,10},{16,20},{18,... | collective-permute-start | bytes 1376264 | tf_op jit(solution)/shard_map/ppermute | solution.py:36
  155.2 27.4 %collective-permute-start.13 = (bf16[2,2,32,3584]{3,2,1,0:T(8,128)(2,1)S(1)}, bf16[2,2,32,3584]{3,2,1,0:T(8,128)(2,1)S(1)}, u32[]{:S(2)}, u32[]{:S(2)}) collective-permute-start(bf16[2,2,32,3584]{3,2,1,0:T(8,128)(2,1)S(1)} %collective-permute-done.5), channel_id=1, source_target_pairs={{8,0},{10,2},{12,4},{14,6},{9,1},{11,3},{13,5},{15,7}} | collective-permute-start | bytes 2752520 | tf_op jit(solution)/shard_map/ppermute | solution.py:36
  156.5 32.0 %slice-start.2 = ((s8[7340032]{0:T(1024)(128)(4,1)}), s8[4194304]{0:T(1024)(128)(4,1)S(1)}, s32[]{:S(2)}) async-start(s8[7340032]{0:T(1024)(128)(4,1)} %bitcast.228), calls=%async_computation.2 | async-start | bytes 8388608
  158.0 28.6 %copy-start.5 = (bf16[1,4,64,3584]{3,2,1,0:T(8,128)(2,1)S(1)}, bf16[1,4,64,3584]{3,2,1,0:T(8,128)(2,1)}, u32[]{:S(2)}) copy-start(bf16[1,4,64,3584]{3,2,1,0:T(8,128)(2,1)} %param.15) | copy-start | bytes 5505028
  158.1 33.6 %collective-permute-start.11 = (bf16[1,2,32,3584]{3,2,1,0:T(8,128)(2,1)S(1)}, bf16[1,2,32,3584]{3,2,1,0:T(8,128)(2,1)S(1)}, u32[]{:S(2)}, u32[]{:S(2)}) collective-permute-start(bf16[1,2,32,3584]{3,2,1,0:T(8,128)(2,1)S(1)} %get-tuple-element.47), channel_id=1, source_target_pairs={{0,2},{2,0},{4,6},{6,4},{8,10},{10,8},{12,14},{14,12},{16,18},{18,... | collective-permute-start | bytes 1376264 | tf_op jit(solution)/shard_map/ppermute | solution.py:36
  182.7 13.4 %collective-permute-start.12 = (bf16[1,2,32,3584]{3,2,1,0:T(8,128)(2,1)S(1)}, bf16[1,2,32,3584]{3,2,1,0:T(8,128)(2,1)S(1)}, u32[]{:S(2)}, u32[]{:S(2)}) collective-permute-start(bf16[1,2,32,3584]{3,2,1,0:T(8,128)(2,1)S(1)} %get-tuple-element.46), channel_id=1, source_target_pairs={{0,4},{2,6},{4,0},{6,2},{8,12},{10,14},{12,8},{14,10},{16,20},{18,... | collective-permute-start | bytes 1376264 | tf_op jit(solution)/shard_map/ppermute | solution.py:36
  184.6 14.7 %collective-permute-start.14 = (bf16[1,2,32,3584]{3,2,1,0:T(8,128)(2,1)S(1)}, bf16[1,2,32,3584]{3,2,1,0:T(8,128)(2,1)S(1)}, u32[]{:S(2)}, u32[]{:S(2)}) collective-permute-start(bf16[1,2,32,3584]{3,2,1,0:T(8,128)(2,1)S(1)} %get-tuple-element.45), channel_id=1, source_target_pairs={{0,2},{2,0},{4,6},{6,4},{8,10},{10,8},{12,14},{14,12},{16,18},{18,... | collective-permute-start | bytes 1376264 | tf_op jit(solution)/shard_map/ppermute | solution.py:36
  186.3 16.0 %collective-permute-start.15 = (bf16[1,2,32,3584]{3,2,1,0:T(8,128)(2,1)S(1)}, bf16[1,2,32,3584]{3,2,1,0:T(8,128)(2,1)S(1)}, u32[]{:S(2)}, u32[]{:S(2)}) collective-permute-start(bf16[1,2,32,3584]{3,2,1,0:T(8,128)(2,1)S(1)} %get-tuple-element.44), channel_id=1, source_target_pairs={{0,4},{2,6},{4,0},{6,2},{8,12},{10,14},{12,8},{14,10},{16,20},{18,... | collective-permute-start | bytes 1376264 | tf_op jit(solution)/shard_map/ppermute | solution.py:36
  (7 other events, 49.5 us)
